TPU v7x, 32 devices: a whole 2x2x4 slice. The times are simulated.
32 devices in a mesh: gx: 4 (over z), gy: 8 (over y, x, core).
Axes of the slice: x: 2, y: 2, z: 4, core: 2. Of those that a mesh axis runs over, the one named last changes fastest.
Arguments:
- forcing: float32 [16, 128, 512], P(None, 'gy', 'gx'), may hold values from -6 to 6
- pressure_in: float32 [16, 128, 512], P(None, 'gy', 'gx'), may hold values from -6 to 6
- x_coupling: float32 [16, 128, 512], P(None, 'gy', 'gx'), may hold values from 0.5 to 2000
- y_coupling: float32 [16, 128, 512], P(None, 'gy', 'gx'), may hold values from 0.5 to 2000
- z_coupling: float32 [16, 128, 512], P(None, 'gy', 'gx'), may hold values from 0.05 to 0.5
- damping: float32 [16, 128, 512], P(None, 'gy', 'gx'), may hold values from 0.2 to 2
Outputs:
- pressure: float32 [16, 128, 512], P(None, 'gy', 'gx')
- coarse_residual: float32 [8, 64, 256], P(None, 'gy', 'gx')
- coarse_correction: float32 [8, 64, 256], P(None, 'gy')
All inputs are finite; a program needn't handle non-finite values.
Results may differ from a plain program's by a relative error of at most 0.0001.
Values sent between devices are 32-bit elements; how exact they have to be, the bound alone decides.
A program may use at most 128 MiB of HBM per device.

v0:
```python
import jax
import jax.numpy as jnp
from jax import lax
from jax.sharding import PartitionSpec as P

COARSE = 3


RELAX = 0.8


def extended(value, sides, width):
    for axis, dim in sides:
        peers, length = (lax.axis_size(axis), value.shape[dim])
        up = [(i, (i + 1) % peers) for i in range(peers - 1)]
        down = [(j, i) for i, j in up]
        last = lax.slice_in_dim(value, length - width, length, axis=dim)
        leading = lax.slice_in_dim(value, 0, width, axis=dim)
        before = lax.ppermute(last, axis, up)
        after = lax.ppermute(leading, axis, down)
        value = jnp.concatenate([before, value, after], axis=dim)
    return value


def from_behind(value, axis, steps):
    count = lax.axis_size(axis)
    leading, last = (max(0, -steps), min(count, count - steps))
    return lax.ppermute(value, axis, [(source, source + steps) for source in range(leading, last)])


def shifted(values, offset, axis_dim, filler):
    length = values.shape[axis_dim]
    if offset > 0:
        border = jnp.full_like(lax.slice_in_dim(values, 0, offset, axis=axis_dim), filler)
        return jnp.concatenate(
            [border, lax.slice_in_dim(values, 0, length - offset, axis=axis_dim)], axis=axis_dim
        )
    amount = -offset
    border = jnp.full_like(lax.slice_in_dim(values, 0, amount, axis=axis_dim), filler)
    return jnp.concatenate(
        [lax.slice_in_dim(values, amount, length, axis=axis_dim), border], axis=axis_dim
    )


def line_solve(low_band, diagonal, up_band, right_side, axis_dim):
    length = right_side.shape[axis_dim]
    stride = 1
    while stride < length:
        before = shifted(diagonal, stride, axis_dim, 1.0)
        after = shifted(diagonal, -stride, axis_dim, 1.0)
        weight_low = -low_band / before
        weight_up = -up_band / after
        new_diag = (
            diagonal
            + weight_low * shifted(up_band, stride, axis_dim, 0.0)
            + weight_up * shifted(low_band, -stride, axis_dim, 0.0)
        )
        new_right = (
            right_side
            + weight_low * shifted(right_side, stride, axis_dim, 0.0)
            + weight_up * shifted(right_side, -stride, axis_dim, 0.0)
        )
        low_band = weight_low * shifted(low_band, stride, axis_dim, 0.0)
        up_band = weight_up * shifted(up_band, -stride, axis_dim, 0.0)
        diagonal = new_diag
        right_side = new_right
        stride = stride * 2
    return right_side / diagonal


def top_masked(coupling):
    levels = coupling.shape[0]
    keep = (jnp.arange(levels) < levels - 1)[:, None, None]
    return jnp.where(keep, coupling, jnp.zeros_like(coupling))


def vertical(field, z_low, z_top):
    return z_low * shifted(field, 1, 0, 0.0) + z_top * shifted(field, -1, 0, 0.0)


def restrict(field):
    levels, rows, columns = field.shape
    blocks = field.reshape(levels // 2, 2, rows // 2, 2, columns // 2, 2)
    return jnp.sum(blocks, axis=(1, 3, 5)) * 0.125


def y_rim(field):
    return extended(field, (("gy", 1),), 1)


def x_return(solved):
    return lax.all_to_all(solved, "gx", split_axis=2, concat_axis=0, tiled=True)


def y_return(solved):
    return lax.all_to_all(solved, "gy", split_axis=1, concat_axis=0, tiled=True)


def x_solve(diag_lines, band_lines, source_lines):
    return line_solve(-shifted(band_lines, 1, 2, 0.0), diag_lines, -band_lines, source_lines, 2)


def y_solve(diag_lines, band_lines, source_lines):
    return line_solve(-shifted(band_lines, 1, 1, 0.0), diag_lines, -band_lines, source_lines, 1)


def body(forcing, pressure_in, x_coupling, y_coupling, z_coupling, damping):
    z_top = top_masked(z_coupling)
    z_low = shifted(z_top, 1, 0, 0.0)
    x_left = jnp.concatenate(
        [from_behind(x_coupling[:, :, -1:], "gx", 1), x_coupling[:, :, :-1]], axis=2
    )
    y_left = jnp.concatenate(
        [from_behind(y_coupling[:, -1:, :], "gy", 1), y_coupling[:, :-1, :]], axis=1
    )
    diagonal = x_left + x_coupling + y_left + y_coupling + z_low + z_top + damping
    field = pressure_in
    for repeat in range(2):
        padded = y_rim(field)
        source = (
            forcing
            + y_left * padded[:, :-2, :]
            + y_coupling * padded[:, 2:, :]
            + vertical(field, z_low, z_top)
        )
        source_lines, diag_lines, band_lines = (
            lax.all_to_all(source, "gx", split_axis=0, concat_axis=2, tiled=True),
            lax.all_to_all(diagonal, "gx", split_axis=0, concat_axis=2, tiled=True),
            lax.all_to_all(x_coupling, "gx", split_axis=0, concat_axis=2, tiled=True),
        )
        field = x_return(x_solve(diag_lines, band_lines, source_lines))
        padded = extended(field, (("gx", 2),), 1)
        source = (
            forcing
            + x_left * padded[:, :, :-2]
            + x_coupling * padded[:, :, 2:]
            + vertical(field, z_low, z_top)
        )
        source_lines, diag_lines, band_lines = (
            lax.all_to_all(source, "gy", split_axis=0, concat_axis=1, tiled=True),
            lax.all_to_all(diagonal, "gy", split_axis=0, concat_axis=1, tiled=True),
            lax.all_to_all(y_coupling, "gy", split_axis=0, concat_axis=1, tiled=True),
        )
        field = y_return(y_solve(diag_lines, band_lines, source_lines))
    padded = extended(field, (("gy", 1), ("gx", 2)), 1)
    applied = (
        diagonal * field
        - x_left * padded[:, 1:-1, :-2]
        - x_coupling * padded[:, 1:-1, 2:]
        - y_left * padded[:, :-2, 1:-1]
        - y_coupling * padded[:, 2:, 1:-1]
        - vertical(field, z_low, z_top)
    )
    coarse_residual = restrict(forcing - applied)
    coarse_x = restrict(x_coupling)
    coarse_y = restrict(y_coupling)
    coarse_z = restrict(z_coupling)
    coarse_damp = restrict(damping)
    whole_res, whole_x, whole_y, whole_z, whole_damp = (
        lax.all_gather(coarse_residual, "gx", axis=2, tiled=True),
        lax.all_gather(coarse_x, "gx", axis=2, tiled=True),
        lax.all_gather(coarse_y, "gx", axis=2, tiled=True),
        lax.all_gather(coarse_z, "gx", axis=2, tiled=True),
        lax.all_gather(coarse_damp, "gx", axis=2, tiled=True),
    )
    cz_top = top_masked(whole_z)
    cz_low = shifted(cz_top, 1, 0, 0.0)
    cx_left = shifted(whole_x, 1, 2, 0.0)
    cy_left = jnp.concatenate(
        [from_behind(whole_y[:, -1:, :], "gy", 1), whole_y[:, :-1, :]], axis=1
    )
    coarse_diag = cx_left + whole_x + cy_left + whole_y + cz_low + cz_top + whole_damp
    correction = RELAX * whole_res / coarse_diag
    for repeat in range(COARSE - 1):
        padded = extended(correction, (("gy", 1),), 1)
        applied_coarse = (
            coarse_diag * correction
            - cx_left * shifted(correction, 1, 2, 0.0)
            - whole_x * shifted(correction, -1, 2, 0.0)
            - cy_left * padded[:, :-2, :]
            - whole_y * padded[:, 2:, :]
            - vertical(correction, cz_low, cz_top)
        )
        correction = correction + RELAX * (whole_res - applied_coarse) / coarse_diag
    return (field, coarse_residual, correction)


def solution(mesh):
    in_specs = (
        P(None, "gy", "gx"),
        P(None, "gy", "gx"),
        P(None, "gy", "gx"),
        P(None, "gy", "gx"),
        P(None, "gy", "gx"),
        P(None, "gy", "gx"),
    )
    out_specs = (P(None, "gy", "gx"), P(None, "gy", "gx"), P(None, "gy", None))
    return jax.shard_map(body, mesh=mesh, in_specs=in_specs, out_specs=out_specs, check_vma=False)
```

profile of v0, /device:TPU:1, one launch (start us, length us, event | category | flops | bytes accessed | tf_op | source)
XLA Modules:
  0.0 383.3 jit_solution(15006799556907630283)
XLA Ops:
  0.6 5.4 %all-to-all-start.1 = ((f32[16,16,128]{2,1,0:T(8,128)}), f32[16,16,128]{2,1,0:T(8,128)S(1)}, u32[]{:S(2)}, u32[]{:S(2)}) async-start(f32[16,16,128]{2,1,0:T(8,128)} %param.8), calls=%async_computation.1 | async-start | bytes 262144 | tf_op jit(solution)/shard_map/all_to_all | solution.py:129
  6.9 4.0 %collective-permute-start.2 = (f32[16,1,128]{2,1,0:T(1,128)S(1)}, f32[16,1,128]{2,1,0:T(1,128)S(1)}, u32[]{:S(2)}, u32[]{:S(2)}) collective-permute-start(f32[16,1,128]{2,1,0:T(1,128)S(1)} %get-tuple-element.265), channel_id=1, source_target_pairs={{0,1},{1,2},{2,3},{3,4},{4,5},{5,6},{6,7},{8,9},{9,10},{10,11},{11... | collective-permute-start | bytes 24584 | tf_op jit(solution)/shard_map/ppermute | solution.py:19
  26.7 9.6 %all_to_all.236 = f32[16,16,128]{2,1,0:T(8,128)S(1)} all-to-all(f32[16,16,128]{2,1,0:T(8,128)S(1)} %get-tuple-element.78), channel_id=1, replica_groups=mesh['gx'=4,'gy'=8] {'gx'}, dimensions={0} | all-to-all | bytes 262144 | tf_op jit(solution)/shard_map/all_to_all | solution.py:127
  40.2 4.5 %all-to-all-done.2 = f32[16,16,128]{2,1,0:T(8,128)S(1)} async-done(((f32[16,16,128]{2,1,0:T(8,128)}), f32[16,16,128]{2,1,0:T(8,128)S(1)}, u32[]{:S(2)}, u32[]{:S(2)}) %all-to-all-start.2) | async-done | bytes 131104 | tf_op jit(solution)/shard_map/all_to_all | solution.py:128
  44.7 6.6 %all-to-all-start.5 = ((f32[16,16,128]{2,1,0:T(8,128)}), f32[16,16,128]{2,1,0:T(8,128)S(1)}, u32[]{:S(2)}, u32[]{:S(2)}) async-start(f32[16,16,128]{2,1,0:T(8,128)} %param.9), calls=%async_computation.5 | async-start | bytes 262144 | tf_op jit(solution)/shard_map/all_to_all | solution.py:142
  57.6 4.2 %all-to-all-start.6 = ((f32[16,16,128]{2,1,0:T(8,128)}), f32[16,16,128]{2,1,0:T(8,128)S(1)}, u32[]{:S(2)}, u32[]{:S(2)}) async-start(f32[16,16,128]{2,1,0:T(8,128)} %get-tuple-element.76), calls=%async_computation.6 | async-start | bytes 262144 | tf_op jit(solution)/shard_map/all_to_all | solution.py:141
  69.7 9.7 %reshape.31 = f32[8,2,8,2,64,2]{5,4,3,2,1,0:T(8,128)} reshape(f32[16,16,128]{2,1,0:T(8,128)S(1)} %copy-done) | data formatting | bytes 262144 | tf_op jit(solution)/shard_map/reshape | solution.py:83
  79.5 4.7 %reduce_sum.47 = f32[8,8,64]{2,1,0:T(8,128)} reduce(f32[8,2,8,2,64,2]{5,4,3,2,1,0:T(8,128)} %reshape.31, f32[]{:T(128)} %constant.7.clone.1), dimensions={1,3,5}, to_apply=%region_2.3 | reduce | flops 28672 | bytes 147460 | tf_op jit(solution)/shard_map/reduce_sum | solution.py:84
  96.8 6.0 %all-to-all-start.4 = ((f32[16,16,128]{2,1,0:T(8,128)}), f32[16,16,128]{2,1,0:T(8,128)S(1)}, u32[]{:S(2)}, u32[]{:S(2)}) async-start(f32[16,16,128]{2,1,0:T(8,128)} %fusion.22), calls=%async_computation.4 | async-start | bytes 262144 | tf_op jit(solution)/shard_map/all_to_all | solution.py:140
  102.7 4.6 %all-to-all-done.4 = f32[16,16,128]{2,1,0:T(8,128)S(1)} async-done(((f32[16,16,128]{2,1,0:T(8,128)}), f32[16,16,128]{2,1,0:T(8,128)S(1)}, u32[]{:S(2)}, u32[]{:S(2)}) %all-to-all-start.4) | async-done | bytes 131104 | tf_op jit(solution)/shard_map/all_to_all | solution.py:140
  111.2 5.0 %all-to-all-start.7 = ((f32[2,128,128]{2,0,1:T(2,128)}), f32[2,128,128]{2,0,1:T(2,128)}, u32[]{:S(2)}, u32[]{:S(2)}) async-start(f32[2,128,128]{2,0,1:T(2,128)} %copy.192), calls=%async_computation.7 | async-start | bytes 262144 | tf_op jit(solution)/shard_map/all_to_all | solution.py:96
  116.4 20.5 %all_gather.17 = f32[8,8,256]{1,0,2:T(8,128)S(1)} all-gather(f32[8,8,64]{1,0,2:T(8,128)S(1)} %copy.208), channel_id=1, replica_groups=mesh['gx'=4,'gy'=8] {'gx'}, dimensions={2}, use_global_device_ids=true | all-gather | bytes 81920 | tf_op jit(solution)/shard_map/all_gather | solution.py:162
  137.7 4.8 %collective-permute-start.14 = (f32[8,1,256]{2,0,1:T(8,128)S(1)}, f32[8,1,256]{2,0,1:T(8,128)}, u32[]{:S(2)}, u32[]{:S(2)}) collective-permute-start(f32[8,1,256]{2,0,1:T(8,128)S(1)} %copy.209), channel_id=1, source_target_pairs={{0,1},{1,2},{2,3},{3,4},{4,5},{5,6},{6,7},{8,9},{9,10},{10,11},{11... | collective-permute-start | bytes 24584 | tf_op jit(solution)/shard_map/ppermute | solution.py:28
  142.5 9.7 %reshape.32 = f32[8,2,8,2,64,2]{5,4,3,2,1,0:T(8,128)} reshape(f32[16,16,128]{2,1,0:T(8,128)S(1)} %copy-done.2) | data formatting | bytes 262144 | tf_op jit(solution)/shard_map/reshape | solution.py:83
  152.2 4.0 %reduce_sum.48 = f32[8,8,64]{2,1,0:T(8,128)S(1)} reduce(f32[8,2,8,2,64,2]{5,4,3,2,1,0:T(8,128)} %reshape.32, f32[]{:T(128)} %constant.7.clone.1), dimensions={1,3,5}, to_apply=%region_3.4 | reduce | flops 28672 | bytes 147460 | tf_op jit(solution)/shard_map/reduce_sum | solution.py:84
  168.8 9.7 %reshape.33 = f32[8,2,8,2,64,2]{5,4,3,2,1,0:T(8,128)} reshape(f32[16,16,128]{2,1,0:T(8,128)S(1)} %copy-done.51) | data formatting | bytes 262144 | tf_op jit(solution)/shard_map/reshape | solution.py:83
  178.6 9.7 %reshape.30 = f32[8,2,8,2,64,2]{5,4,3,2,1,0:T(8,128)} reshape(f32[16,16,128]{2,1,0:T(8,128)S(1)} %copy-done.1) | data formatting | bytes 262144 | tf_op jit(solution)/shard_map/reshape | solution.py:83
  188.3 4.6 %reduce_sum.49 = f32[8,8,64]{2,1,0:T(8,128)} reduce(f32[8,2,8,2,64,2]{5,4,3,2,1,0:T(8,128)} %reshape.33, f32[]{:T(128)} %constant.7.clone.1), dimensions={1,3,5}, to_apply=%region_4.5 | reduce | flops 28672 | bytes 147460 | tf_op jit(solution)/shard_map/reduce_sum | solution.py:84
  193.7 21.1 %all_gather.18 = f32[8,8,256]{1,0,2:T(8,128)S(1)} all-gather(f32[8,8,64]{1,0,2:T(8,128)} %copy.213), channel_id=1, replica_groups=mesh['gx'=4,'gy'=8] {'gx'}, dimensions={2}, use_global_device_ids=true | all-gather | bytes 81920 | tf_op jit(solution)/shard_map/all_gather | solution.py:163
  215.8 4.7 %reduce_sum.46 = f32[8,8,64]{2,1,0:T(8,128)} reduce(f32[8,2,8,2,64,2]{5,4,3,2,1,0:T(8,128)} %reshape.30, f32[]{:T(128)} %constant.7.clone.1), dimensions={1,3,5}, to_apply=%region_1.2 | reduce | flops 28672 | bytes 147460 | tf_op jit(solution)/shard_map/reduce_sum | solution.py:84
  226.3 4.6 %all-to-all-start.9 = ((f32[4,1,8192]{2,1,0:T(1,128)}), f32[4,1,8192]{2,1,0:T(1,128)S(1)}, u32[]{:S(2)}, u32[]{:S(2)}) async-start(f32[4,1,8192]{2,1,0:T(1,128)} %reshape.36), calls=%async_computation.9 | async-start | bytes 262144 | tf_op jit(solution)/shard_map/all_to_all | solution.py:92
  248.6 6.7 %all-to-all-start.10 = ((f32[16,16,128]{2,1,0:T(8,128)}), f32[16,16,128]{2,1,0:T(8,128)S(1)}, u32[]{:S(2)}, u32[]{:S(2)}) async-start(f32[16,16,128]{2,1,0:T(8,128)} %fusion.12), calls=%async_computation.10 | async-start | bytes 262144 | tf_op jit(solution)/shard_map/all_to_all | solution.py:140
  264.9 4.2 %all-to-all-start.11 = ((f32[2,128,128]{2,0,1:T(2,128)}), f32[2,128,128]{2,0,1:T(2,128)S(1)}, u32[]{:S(2)}, u32[]{:S(2)}) async-start(f32[2,128,128]{2,0,1:T(2,128)} %copy.200), calls=%async_computation.11 | async-start | bytes 262144 | tf_op jit(solution)/shard_map/all_to_all | solution.py:96
  271.0 20.5 %all_gather.19 = f32[8,8,256]{1,0,2:T(8,128)S(1)} all-gather(f32[8,8,64]{1,0,2:T(8,128)S(1)} %copy.215), channel_id=1, replica_groups=mesh['gx'=4,'gy'=8] {'gx'}, dimensions={2}, use_global_device_ids=true | all-gather | bytes 81920 | tf_op jit(solution)/shard_map/all_gather | solution.py:164
  291.5 4.7 %collective-permute-start.10 = (f32[16,1,128]{2,1,0:T(1,128)S(1)}, f32[16,1,128]{2,1,0:T(1,128)S(1)}, u32[]{:S(2)}, u32[]{:S(2)}) collective-permute-start(f32[16,1,128]{2,1,0:T(1,128)S(1)} %get-tuple-element.83), channel_id=1, source_target_pairs={{0,1},{1,2},{2,3},{3,4},{4,5},{5,6},{6,7},{8,9},{9,10},{10,11},{11... | collective-permute-start | bytes 24584 | tf_op jit(solution)/shard_map/ppermute | solution.py:19
  298.2 19.4 %all_gather.16 = f32[8,8,256]{1,0,2:T(8,128)} all-gather(f32[8,8,64]{1,0,2:T(8,128)S(1)} %copy.205), channel_id=1, replica_groups=mesh['gx'=4,'gy'=8] {'gx'}, dimensions={2}, use_global_device_ids=true | all-gather | bytes 81920 | tf_op jit(solution)/shard_map/all_gather | solution.py:161
  326.1 4.5 %collective-permute-done.13 = f32[16,18,1]{2,1,0:T(8,128)S(1)} collective-permute-done((f32[16,18,1]{2,1,0:T(8,128)S(1)}, f32[16,18,1]{2,1,0:T(8,128)S(1)}, u32[]{:S(2)}, u32[]{:S(2)}) %collective-permute-start.13) | collective-permute-done | bytes 1184 | tf_op jit(solution)/shard_map/ppermute | solution.py:20
  331.8 9.7 %reshape.29 = f32[8,2,8,2,64,2]{5,4,3,2,1,0:T(8,128)} reshape(f32[16,16,128]{2,1,0:T(8,128)S(1)} %fusion.3) | data formatting | bytes 262144 | tf_op jit(solution)/shard_map/reshape | solution.py:83
  341.6 4.0 %reduce_sum.45 = f32[8,8,64]{2,1,0:T(8,128)S(1)} reduce(f32[8,2,8,2,64,2]{5,4,3,2,1,0:T(8,128)} %reshape.29, f32[]{:T(128)} %constant.7.clone.1), dimensions={1,3,5}, to_apply=%region_0.1 | reduce | flops 28672 | bytes 147460 | tf_op jit(solution)/shard_map/reduce_sum | solution.py:84
  345.8 21.4 %all_gather.15 = f32[8,8,256]{1,0,2:T(8,128)S(1)} all-gather(f32[8,8,64]{1,0,2:T(8,128)S(1)} %copy.203), channel_id=1, replica_groups=mesh['gx'=4,'gy'=8] {'gx'}, dimensions={2}, use_global_device_ids=true | all-gather | bytes 81920 | tf_op jit(solution)/shard_map/all_gather | solution.py:160
  370.4 4.2 %collective-permute-start.15 = (f32[8,1,256]{2,0,1:T(8,128)S(1)}, f32[8,1,256]{2,0,1:T(8,128)S(1)}, u32[]{:S(2)}, u32[]{:S(2)}) collective-permute-start(f32[8,1,256]{2,0,1:T(8,128)S(1)} %copy.218), channel_id=1, source_target_pairs={{0,1},{1,2},{2,3},{3,4},{4,5},{5,6},{6,7},{8,9},{9,10},{10,11},{11... | collective-permute-start | bytes 24584 | tf_op jit(solution)/shard_map/ppermute | solution.py:19
  377.6 4.2 %collective-permute-start.17 = (f32[8,1,256]{2,0,1:T(8,128)S(1)}, f32[8,1,256]{2,0,1:T(8,128)S(1)}, u32[]{:S(2)}, u32[]{:S(2)}) collective-permute-start(f32[8,1,256]{2,0,1:T(8,128)S(1)} %copy.225), channel_id=1, source_target_pairs={{0,1},{1,2},{2,3},{3,4},{4,5},{5,6},{6,7},{8,9},{9,10},{10,11},{11... | collective-permute-start | bytes 24584 | tf_op jit(solution)/shard_map/ppermute | solution.py:19
  (422 shorter events, 118.9 us)
Async XLA Ops:
  0.6 26.1 %all-to-all-start.1 = ((f32[16,16,128]{2,1,0:T(8,128)}), f32[16,16,128]{2,1,0:T(8,128)S(1)}, u32[]{:S(2)}, u32[]{:S(2)}) async-start(f32[16,16,128]{2,1,0:T(8,128)} %param.8), calls=%async_computation.1 | async-start | bytes 262144 | tf_op jit(solution)/shard_map/all_to_all | solution.py:129
  6.9 17.6 %collective-permute-start.2 = (f32[16,1,128]{2,1,0:T(1,128)S(1)}, f32[16,1,128]{2,1,0:T(1,128)S(1)}, u32[]{:S(2)}, u32[]{:S(2)}) collective-permute-start(f32[16,1,128]{2,1,0:T(1,128)S(1)} %get-tuple-element.265), channel_id=1, source_target_pairs={{0,1},{1,2},{2,3},{3,4},{4,5},{5,6},{6,7},{8,9},{9,10},{10,11},{11... | collective-permute-start | bytes 24584 | tf_op jit(solution)/shard_map/ppermute | solution.py:19
  10.9 13.6 %collective-permute-start.3 = (f32[16,1,128]{2,1,0:T(1,128)S(1)}, f32[16,1,128]{2,1,0:T(1,128)S(1)}, u32[]{:S(2)}, u32[]{:S(2)}) collective-permute-start(f32[16,1,128]{2,1,0:T(1,128)S(1)} %get-tuple-element.266), channel_id=1, source_target_pairs={{1,0},{2,1},{3,2},{4,3},{5,4},{6,5},{7,6},{9,8},{10,9},{11,10},{12... | collective-permute-start | bytes 24584 | tf_op jit(solution)/shard_map/ppermute | solution.py:20
  13.7 10.8 %collective-permute-start.1 = (f32[16,1,128]{2,1,0:T(1,128)S(1)}, f32[16,1,128]{2,1,0:T(1,128)S(1)}, u32[]{:S(2)}, u32[]{:S(2)}) collective-permute-start(f32[16,1,128]{2,1,0:T(1,128)S(1)} %slice.763), channel_id=1, source_target_pairs={{0,1},{1,2},{2,3},{3,4},{4,5},{5,6},{6,7},{8,9},{9,10},{10,11},{11... | collective-permute-start | bytes 24584 | tf_op jit(solution)/shard_map/ppermute | solution.py:28
  18.3 6.2 %collective-permute-start = (f32[16,16,1]{2,1,0:T(8,128)S(1)}, f32[16,16,1]{2,1,0:T(8,128)S(1)}, u32[]{:S(2)}, u32[]{:S(2)}) collective-permute-start(f32[16,16,1]{2,1,0:T(8,128)S(1)} %slice.761), channel_id=1, source_target_pairs={{0,8},{8,16},{16,24},{1,9},{9,17},{17,25},{2,10},{10,18},{18,26},{... | collective-permute-start | bytes 3080 | tf_op jit(solution)/shard_map/ppermute | solution.py:28
  26.7 69.2 %copy-start.15 = (f32[16,16,128]{2,1,0:T(8,128)}, f32[16,16,128]{2,1,0:T(8,128)S(1)}, u32[]{:S(2)}) copy-start(f32[16,16,128]{2,1,0:T(8,128)S(1)} %get-tuple-element.77) | copy-start | bytes 393220
  36.3 8.3 %all-to-all-start.2 = ((f32[16,16,128]{2,1,0:T(8,128)}), f32[16,16,128]{2,1,0:T(8,128)S(1)}, u32[]{:S(2)}, u32[]{:S(2)}) async-start(f32[16,16,128]{2,1,0:T(8,128)} %get-tuple-element.76), calls=%async_computation.2 | async-start | bytes 262144 | tf_op jit(solution)/shard_map/all_to_all | solution.py:128
  44.7 12.9 %all-to-all-start.5 = ((f32[16,16,128]{2,1,0:T(8,128)}), f32[16,16,128]{2,1,0:T(8,128)S(1)}, u32[]{:S(2)}, u32[]{:S(2)}) async-start(f32[16,16,128]{2,1,0:T(8,128)} %param.9), calls=%async_computation.5 | async-start | bytes 262144 | tf_op jit(solution)/shard_map/all_to_all | solution.py:142
  57.6 8.7 %all-to-all-start.6 = ((f32[16,16,128]{2,1,0:T(8,128)}), f32[16,16,128]{2,1,0:T(8,128)S(1)}, u32[]{:S(2)}, u32[]{:S(2)}) async-start(f32[16,16,128]{2,1,0:T(8,128)} %get-tuple-element.76), calls=%async_computation.6 | async-start | bytes 262144 | tf_op jit(solution)/shard_map/all_to_all | solution.py:141
  66.4 17.9 %all-to-all-start.3 = ((f32[4,1,8192]{2,1,0:T(1,128)}), f32[4,1,8192]{2,1,0:T(1,128)S(1)}, u32[]{:S(2)}, u32[]{:S(2)}) async-start(f32[4,1,8192]{2,1,0:T(1,128)} %reshape.34), calls=%async_computation.3 | async-start | bytes 262144 | tf_op jit(solution)/shard_map/all_to_all | solution.py:92
  86.8 5.2 %collective-permute-start.4 = (f32[16,16,1]{2,1,0:T(8,128)S(1)}, f32[16,16,1]{2,1,0:T(8,128)S(1)}, u32[]{:S(2)}, u32[]{:S(2)}) collective-permute-start(f32[16,16,1]{2,1,0:T(8,128)S(1)} %get-tuple-element.186), channel_id=1, source_target_pairs={{0,8},{8,16},{16,24},{1,9},{9,17},{17,25},{2,10},{10,18},{18,26},{... | collective-permute-start | bytes 3080 | tf_op jit(solution)/shard_map/ppermute | solution.py:19
  90.2 5.7 %collective-permute-start.5 = (f32[16,16,1]{2,1,0:T(8,128)S(1)}, f32[16,16,1]{2,1,0:T(8,128)S(1)}, u32[]{:S(2)}, u32[]{:S(2)}) collective-permute-start(f32[16,16,1]{2,1,0:T(8,128)S(1)} %get-tuple-element.187), channel_id=1, source_target_pairs={{8,0},{16,8},{24,16},{9,1},{17,9},{25,17},{10,2},{18,10},{26,18},{... | collective-permute-start | bytes 3080 | tf_op jit(solution)/shard_map/ppermute | solution.py:20
  96.8 10.5 %all-to-all-start.4 = ((f32[16,16,128]{2,1,0:T(8,128)}), f32[16,16,128]{2,1,0:T(8,128)S(1)}, u32[]{:S(2)}, u32[]{:S(2)}) async-start(f32[16,16,128]{2,1,0:T(8,128)} %fusion.22), calls=%async_computation.4 | async-start | bytes 262144 | tf_op jit(solution)/shard_map/all_to_all | solution.py:140
  111.2 45.1 %all-to-all-start.7 = ((f32[2,128,128]{2,0,1:T(2,128)}), f32[2,128,128]{2,0,1:T(2,128)}, u32[]{:S(2)}, u32[]{:S(2)}) async-start(f32[2,128,128]{2,0,1:T(2,128)} %copy.192), calls=%async_computation.7 | async-start | bytes 262144 | tf_op jit(solution)/shard_map/all_to_all | solution.py:96
  137.7 183.1 %collective-permute-start.14 = (f32[8,1,256]{2,0,1:T(8,128)S(1)}, f32[8,1,256]{2,0,1:T(8,128)}, u32[]{:S(2)}, u32[]{:S(2)}) collective-permute-start(f32[8,1,256]{2,0,1:T(8,128)S(1)} %copy.209), channel_id=1, source_target_pairs={{0,1},{1,2},{2,3},{3,4},{4,5},{5,6},{6,7},{8,9},{9,10},{10,11},{11... | collective-permute-start | bytes 24584 | tf_op jit(solution)/shard_map/ppermute | solution.py:28
  157.2 4.4 %collective-permute-start.6 = (f32[16,1,128]{2,1,0:T(1,128)S(1)}, f32[16,1,128]{2,1,0:T(1,128)S(1)}, u32[]{:S(2)}, u32[]{:S(2)}) collective-permute-start(f32[16,1,128]{2,1,0:T(1,128)S(1)} %get-tuple-element.123), channel_id=1, source_target_pairs={{0,1},{1,2},{2,3},{3,4},{4,5},{5,6},{6,7},{8,9},{9,10},{10,11},{11... | collective-permute-start | bytes 24584 | tf_op jit(solution)/shard_map/ppermute | solution.py:19
  159.2 5.0 %collective-permute-start.7 = (f32[16,1,128]{2,1,0:T(1,128)S(1)}, f32[16,1,128]{2,1,0:T(1,128)S(1)}, u32[]{:S(2)}, u32[]{:S(2)}) collective-permute-start(f32[16,1,128]{2,1,0:T(1,128)S(1)} %get-tuple-element.124), channel_id=1, source_target_pairs={{1,0},{2,1},{3,2},{4,3},{5,4},{6,5},{7,6},{9,8},{10,9},{11,10},{12... | collective-permute-start | bytes 24584 | tf_op jit(solution)/shard_map/ppermute | solution.py:20
  164.9 55.6 %all-to-all-start.8 = ((f32[16,16,128]{2,1,0:T(8,128)}), f32[16,16,128]{2,1,0:T(8,128)}, u32[]{:S(2)}, u32[]{:S(2)}) async-start(f32[16,16,128]{2,1,0:T(8,128)} %fusion.17), calls=%async_computation.8 | async-start | bytes 262144 | tf_op jit(solution)/shard_map/all_to_all | solution.py:127
  226.3 9.5 %all-to-all-start.9 = ((f32[4,1,8192]{2,1,0:T(1,128)}), f32[4,1,8192]{2,1,0:T(1,128)S(1)}, u32[]{:S(2)}, u32[]{:S(2)}) async-start(f32[4,1,8192]{2,1,0:T(1,128)} %reshape.36), calls=%async_computation.9 | async-start | bytes 262144 | tf_op jit(solution)/shard_map/all_to_all | solution.py:92
  237.9 5.2 %collective-permute-start.8 = (f32[16,16,1]{2,1,0:T(8,128)S(1)}, f32[16,16,1]{2,1,0:T(8,128)S(1)}, u32[]{:S(2)}, u32[]{:S(2)}) collective-permute-start(f32[16,16,1]{2,1,0:T(8,128)S(1)} %get-tuple-element.101), channel_id=1, source_target_pairs={{0,8},{8,16},{16,24},{1,9},{9,17},{17,25},{2,10},{10,18},{18,26},{... | collective-permute-start | bytes 3080 | tf_op jit(solution)/shard_map/ppermute | solution.py:19
  241.1 5.7 %collective-permute-start.9 = (f32[16,16,1]{2,1,0:T(8,128)S(1)}, f32[16,16,1]{2,1,0:T(8,128)S(1)}, u32[]{:S(2)}, u32[]{:S(2)}) collective-permute-start(f32[16,16,1]{2,1,0:T(8,128)S(1)} %get-tuple-element.102), channel_id=1, source_target_pairs={{8,0},{16,8},{24,16},{9,1},{17,9},{25,17},{10,2},{18,10},{26,18},{... | collective-permute-start | bytes 3080 | tf_op jit(solution)/shard_map/ppermute | solution.py:20
  248.6 11.2 %all-to-all-start.10 = ((f32[16,16,128]{2,1,0:T(8,128)}), f32[16,16,128]{2,1,0:T(8,128)S(1)}, u32[]{:S(2)}, u32[]{:S(2)}) async-start(f32[16,16,128]{2,1,0:T(8,128)} %fusion.12), calls=%async_computation.10 | async-start | bytes 262144 | tf_op jit(solution)/shard_map/all_to_all | solution.py:140
  260.8 69.8 %copy-start.16 = (f32[16,16,128]{2,1,0:T(8,128)S(1)}, f32[16,16,128]{2,1,0:T(8,128)}, u32[]{:S(2)}) copy-start(f32[16,16,128]{2,1,0:T(8,128)} %copy-done.15) | copy-start | bytes 393220
  264.9 26.5 %all-to-all-start.11 = ((f32[2,128,128]{2,0,1:T(2,128)}), f32[2,128,128]{2,0,1:T(2,128)S(1)}, u32[]{:S(2)}, u32[]{:S(2)}) async-start(f32[2,128,128]{2,0,1:T(2,128)} %copy.200), calls=%async_computation.11 | async-start | bytes 262144 | tf_op jit(solution)/shard_map/all_to_all | solution.py:96
  291.5 29.9 %collective-permute-start.10 = (f32[16,1,128]{2,1,0:T(1,128)S(1)}, f32[16,1,128]{2,1,0:T(1,128)S(1)}, u32[]{:S(2)}, u32[]{:S(2)}) collective-permute-start(f32[16,1,128]{2,1,0:T(1,128)S(1)} %get-tuple-element.83), channel_id=1, source_target_pairs={{0,1},{1,2},{2,3},{3,4},{4,5},{5,6},{6,7},{8,9},{9,10},{10,11},{11... | collective-permute-start | bytes 24584 | tf_op jit(solution)/shard_map/ppermute | solution.py:19
  296.3 25.2 %collective-permute-start.11 = (f32[16,1,128]{2,1,0:T(1,128)S(1)}, f32[16,1,128]{2,1,0:T(1,128)S(1)}, u32[]{:S(2)}, u32[]{:S(2)}) collective-permute-start(f32[16,1,128]{2,1,0:T(1,128)S(1)} %get-tuple-element.84), channel_id=1, source_target_pairs={{1,0},{2,1},{3,2},{4,3},{5,4},{6,5},{7,6},{9,8},{10,9},{11,10},{12... | collective-permute-start | bytes 24584 | tf_op jit(solution)/shard_map/ppermute | solution.py:20
  321.6 4.5 %collective-permute-start.12 = (f32[16,18,1]{2,1,0:T(8,128)S(1)}, f32[16,18,1]{2,1,0:T(8,128)S(1)}, u32[]{:S(2)}, u32[]{:S(2)}) collective-permute-start(f32[16,18,1]{2,1,0:T(8,128)S(1)} %get-tuple-element.79), channel_id=1, source_target_pairs={{0,8},{8,16},{16,24},{1,9},{9,17},{17,25},{2,10},{10,18},{18,26},{... | collective-permute-start | bytes 3464 | tf_op jit(solution)/shard_map/ppermute | solution.py:19
  323.0 7.6 %collective-permute-start.13 = (f32[16,18,1]{2,1,0:T(8,128)S(1)}, f32[16,18,1]{2,1,0:T(8,128)S(1)}, u32[]{:S(2)}, u32[]{:S(2)}) collective-permute-start(f32[16,18,1]{2,1,0:T(8,128)S(1)} %get-tuple-element.80), channel_id=1, source_target_pairs={{8,0},{16,8},{24,16},{9,1},{17,9},{25,17},{10,2},{18,10},{26,18},{... | collective-permute-start | bytes 3464 | tf_op jit(solution)/shard_map/ppermute | solution.py:20
  367.7 6.9 %collective-permute-start.16 = (f32[8,1,256]{2,0,1:T(8,128)S(1)}, f32[8,1,256]{2,0,1:T(8,128)S(1)}, u32[]{:S(2)}, u32[]{:S(2)}) collective-permute-start(f32[8,1,256]{2,0,1:T(8,128)S(1)} %copy.220), channel_id=1, source_target_pairs={{1,0},{2,1},{3,2},{4,3},{5,4},{6,5},{7,6},{9,8},{10,9},{11,10},{12... | collective-permute-start | bytes 24584 | tf_op jit(solution)/shard_map/ppermute | solution.py:20
  370.4 5.0 %collective-permute-start.15 = (f32[8,1,256]{2,0,1:T(8,128)S(1)}, f32[8,1,256]{2,0,1:T(8,128)S(1)}, u32[]{:S(2)}, u32[]{:S(2)}) collective-permute-start(f32[8,1,256]{2,0,1:T(8,128)S(1)} %copy.218), channel_id=1, source_target_pairs={{0,1},{1,2},{2,3},{3,4},{4,5},{5,6},{6,7},{8,9},{9,10},{10,11},{11... | collective-permute-start | bytes 24584 | tf_op jit(solution)/shard_map/ppermute | solution.py:19
  375.7 6.1 %collective-permute-start.18 = (f32[8,1,256]{2,0,1:T(8,128)S(1)}, f32[8,1,256]{2,0,1:T(8,128)S(1)}, u32[]{:S(2)}, u32[]{:S(2)}) collective-permute-start(f32[8,1,256]{2,0,1:T(8,128)S(1)} %copy.227), channel_id=1, source_target_pairs={{1,0},{2,1},{3,2},{4,3},{5,4},{6,5},{7,6},{9,8},{10,9},{11,10},{12... | collective-permute-start | bytes 24584 | tf_op jit(solution)/shard_map/ppermute | solution.py:20
  377.6 5.0 %collective-permute-start.17 = (f32[8,1,256]{2,0,1:T(8,128)S(1)}, f32[8,1,256]{2,0,1:T(8,128)S(1)}, u32[]{:S(2)}, u32[]{:S(2)}) collective-permute-start(f32[8,1,256]{2,0,1:T(8,128)S(1)} %copy.225), channel_id=1, source_target_pairs={{0,1},{1,2},{2,3},{3,4},{4,5},{5,6},{6,7},{8,9},{9,10},{10,11},{11... | collective-permute-start | bytes 24584 | tf_op jit(solution)/shard_map/ppermute | solution.py:19
  (78 other events, 1033.2 us)
where the time goes:
time: 387 us; the launch traced here: 383 us
  blocking collectives  113 us (29%)
  starting transfers between devices  107 us (28%)
  local copies, waits for them, and re-layouts  77.1 us (20%)
  other arithmetic  45.6 us (12%)
  waiting for transfers between devices  37.7 us (10%)
    reshape x5, local copies, waits for them, and re-layouts, restrict(): blocks = field.reshape(levels // 2, 2, rows // 2, 2, columns // 2, 2)  48.6 us
    ppermute x8, starting transfers between devices, extended(): before = lax.ppermute(last, axis, up)  26.9 us
    reduce_sum x5, other arithmetic, restrict(): return jnp.sum(blocks, axis=(1, 3, 5)) * 0.125  22 us
    all_gather x1, blocking collectives, body(): lax.all_gather(coarse_residual, 'gx', axis=2, tiled=True)  21.4 us
    all_gather x1, blocking collectives, body(): lax.all_gather(coarse_z, 'gx', axis=2, tiled=True)  21.1 us
    all_gather x1, blocking collectives, body(): lax.all_gather(coarse_y, 'gx', axis=2, tiled=True)  20.5 us
    all_gather x1, blocking collectives, body(): lax.all_gather(coarse_damp, 'gx', axis=2, tiled=True)  20.5 us
    all_gather x1, blocking collectives, body(): lax.all_gather(coarse_x, 'gx', axis=2, tiled=True)  19.4 us
  transfers between devices with their start and end apart: 30, of which 15 were waited for; matrix products, arithmetic and copies ran while one was open for 26% of the time, Pallas kernels for 0%

commit v1 on v0

v1 whole, which is shorter than its diff:
```python
import functools

import jax
import jax.numpy as jnp
from jax import lax
from jax.experimental import pallas as pl
from jax.experimental.pallas import tpu as pltpu
from jax.sharding import PartitionSpec as P

COARSE = 3
RELAX = 0.8
MESH = pl.DeviceIdType.MESH


def up(v, s, fill):
    return jnp.concatenate([jnp.full_like(v[:s], fill), v[:-s]], axis=0)


def down(v, s, fill):
    return jnp.concatenate([v[s:], jnp.full_like(v[:s], fill)], axis=0)


def strides_of(length):
    out, s = [], 1
    while s < length:
        out.append(s)
        s *= 2
    return out


class Comm:
    def __init__(self, send_sems):
        self.sems, self.used, self.pending = send_sems, 0, []

    def send(self, src, dst, recv, dev, cond=None):
        copy = pltpu.make_async_remote_copy(
            src_ref=src, dst_ref=dst, send_sem=self.sems.at[self.used], recv_sem=recv,
            device_id=dev, device_id_type=MESH,
        )
        self.used += 1
        self.pending.append((copy, cond))
        if cond is None:
            copy.start()
        else:
            pl.when(cond)(copy.start)

    def finish(self):
        for copy, cond in self.pending:
            if cond is None:
                copy.wait_send()
            else:
                pl.when(cond)(copy.wait_send)


def await_recv(src, dst, sems, recv, dev, cond=None):
    copy = pltpu.make_async_remote_copy(
        src_ref=src, dst_ref=dst, send_sem=sems.at[0], recv_sem=recv, device_id=dev, device_id_type=MESH
    )
    if cond is None:
        copy.wait_recv()
    else:
        pl.when(cond)(copy.wait_recv)


def interface_factor(n, me, ls, le, rs, re, own, tau, sig, bet, tau2, sig2, dlt, kk):
    beta = jnp.zeros_like(ls[0])
    for d in range(n):
        bet[d] = beta
        w = 1.0 / (1.0 - ls[d] * beta)
        t = le[d] * w
        tau[d] = t
        s = t * beta
        sig[d] = s
        beta = re[d] + s * rs[d]
    delta = jnp.zeros_like(ls[0])
    for d in reversed(range(n)):
        dlt[d] = delta
        w = 1.0 / (1.0 - re[d] * delta)
        t = rs[d] * w
        tau2[d] = t
        s = t * delta
        sig2[d] = s
        delta = ls[d] + s * le[d]
    ls_m, le_m, rs_m, re_m = own
    beta, delta = bet[me], dlt[me]
    a, b = 1.0 - beta * ls_m, 1.0 - delta * re_m
    o1, o2 = beta * rs_m, delta * le_m
    inv = 1.0 / (a * b - o1 * o2)
    kk[0], kk[1], kk[2], kk[3] = b * inv, o1 * inv, a * inv, o2 * inv
    kk[4], kk[5] = beta, delta


def interface_solve(n, me, h_left, h_right, gs, ge, tau, tau2, kk):
    alpha = jnp.zeros_like(gs)
    for d in range(n - 1):
        alpha = jnp.where(d < me, h_left(d) + tau[d] * alpha, alpha)
    gamma = jnp.zeros_like(gs)
    for d in reversed(range(1, n)):
        gamma = jnp.where(d > me, h_right(d) + tau2[d] * gamma, gamma)
    p = alpha + kk[4] * gs
    q = gamma + kk[5] * ge
    return kk[0] * p + kk[1] * q, kk[2] * q + kk[3] * p


def kernel(nx, ny, f_ref, p_ref, x_ref, y_ref, z_ref, d_ref, op_ref, or_ref, oc_ref,
           xl_s, xc_s, yl_s, yc_s, zl_s, zt_s, fo_s, p_s, ri_s, g_s, q_s,
           lx_s, rx_s, wx_s, ly_s, ry_s, wy_s,
           sx0, sy0, hx, hyd, hyu, xb, sxb, ycb, syc, yb, shy,
           xtau, xsig, xbet, xtau2, xsig2, xdlt, xkk,
           ytau, ysig, ybet, ytau2, ysig2, ydlt, ykk,
           pair_s, cown, cbuf, rown, rbuf, corr, flip,
           ssem, s0, sx, syco, sy, sc, sr):
    Y, Z, X = xc_s.shape
    CY, CZ = Y // 2, Z // 2
    gx, gy = lax.axis_index("gx"), lax.axis_index("gy")
    has_w, has_e = gx > 0, gx < nx - 1
    has_n, has_s = gy > 0, gy < ny - 1
    west, east = jnp.maximum(gx - 1, 0), jnp.minimum(gx + 1, nx - 1)
    north, south = jnp.maximum(gy - 1, 0), jnp.minimum(gy + 1, ny - 1)
    x_peers = [lax.rem(gx + o, nx) for o in range(1, nx)]
    y_peers = [lax.rem(gy + o, ny) for o in range(1, ny)]

    barrier = pltpu.get_barrier_semaphore()

    def greet(dev):
        pl.semaphore_signal(barrier, inc=1, device_id=dev, device_id_type=MESH)

    for i in x_peers:
        greet((i, gy))
    for j in y_peers:
        greet((gx, j))

    @pl.when(has_n)
    def _():
        for i in x_peers:
            greet((i, north))

    @pl.when(has_s)
    def _():
        for i in x_peers:
            greet((i, south))

    lane = lax.broadcasted_iota(jnp.int32, (Z, X), 1)
    level = lax.broadcasted_iota(jnp.int32, (Z, X), 0)
    lane3 = lax.broadcasted_iota(jnp.int32, (1, 1, X), 2)

    def rows(ref, j):
        return ref[pl.ds(j, Z, stride=Y), :]

    packed = jnp.zeros((Z, X), jnp.float32)
    for j in range(Y):
        v = rows(x_ref, j)
        xc_s[j] = v
        packed = jnp.where(lane == j, v[:, X - 1:], packed)
        yc_s[j] = rows(y_ref, j)
        zv = jnp.where(level < Z - 1, rows(z_ref, j), 0.0)
        zt_s[j] = zv
        zl_s[j] = pltpu.roll(zv, 1, 0)
        fo_s[j] = rows(f_ref, j)
        p_s[j] = rows(p_ref, j)
    sx0[...] = packed
    sy0[0] = yc_s[Y - 1]
    sy0[1] = p_s[Y - 1]
    sy0[2] = p_s[0]

    @pl.when(jnp.logical_not(has_w))
    def _():
        hx[...] = jnp.zeros_like(hx)

    @pl.when(jnp.logical_not(has_n))
    def _():
        hyd[...] = jnp.zeros_like(hyd)
        for d in range(nx):
            cbuf[d, :, 0:3] = jnp.zeros_like(cbuf[d, :, 0:3])
            rbuf[d, 0:2] = jnp.zeros_like(rbuf[d, 0:2])

    @pl.when(jnp.logical_not(has_s))
    def _():
        hyu[...] = jnp.zeros_like(hyu)
        for d in range(nx):
            cbuf[d, :, 3 + CY:] = jnp.zeros_like(cbuf[d, :, 3 + CY:])
            rbuf[d, 2 + CY:] = jnp.zeros_like(rbuf[d, 2 + CY:])

    both = has_n.astype(jnp.int32) + has_s.astype(jnp.int32)
    pl.semaphore_wait(barrier, (nx - 1) + (ny - 1) + (nx - 1) * both)

    comm = Comm(ssem)
    comm.send(sx0, hx, s0.at[0], (east, gy), has_e)
    comm.send(sy0.at[0:2], hyd, s0.at[1], (gx, south), has_s)
    comm.send(sy0.at[2:3], hyu, s0.at[2], (gx, north), has_n)

    half = X // 2
    off = lax.rem(gx, 2) * half
    ii = lax.broadcasted_iota(jnp.int32, (X, X), 0)
    mm = lax.broadcasted_iota(jnp.int32, (X, X), 1)

    def selection(step, start):
        target = lax.rem((ii + (step + 2)) // 2 - 1 + start + X, X)
        return jnp.where(mm == target, 0.125, 0.0)

    def pairs(field):
        v = field.reshape(CY, 2, Z, X)
        pair_s[...] = (v[:, 0] + v[:, 1]).reshape(CY * Z, X)
        return pair_s[pl.ds(0, CY * CZ, stride=2), :] + pair_s[pl.ds(1, CY * CZ, stride=2), :]

    def mxu(a, b):
        return jnp.dot(a, b, precision=lax.Precision.HIGHEST, preferred_element_type=jnp.float32)

    here, there = selection(0, off), selection(0, half - off)
    sel2 = jnp.concatenate([here, there], axis=0)
    zfull = jnp.stack([rows(z_ref, j) for j in range(Y)])
    damp = jnp.stack([rows(d_ref, j) for j in range(Y)])
    for m, (u, v) in enumerate(((xc_s[...], yc_s[...]), (zfull, damp))):
        both_pairs = jnp.concatenate([pairs(u), pairs(v)], axis=1)
        cown[m] = mxu(both_pairs, sel2).reshape(CY, CZ, X)

    await_recv(sx0, hx, ssem, s0.at[0], (east, gy), has_w)
    await_recv(sy0.at[0:2], hyd, ssem, s0.at[1], (gx, south), has_n)
    await_recv(sy0.at[2:3], hyu, ssem, s0.at[2], (gx, north), has_s)

    xc, yc = xc_s[...], yc_s[...]
    border = jnp.stack([jnp.broadcast_to(hx[:, j:j + 1], (Z, X)) for j in range(Y)])
    xl = jnp.where(lane3 == 0, border, pltpu.roll(xc, 1, 2))
    xl_s[...] = xl
    yl = jnp.concatenate([hyd[0:1], yc[:-1]], axis=0)
    yl_s[...] = yl
    zd = zl_s[...] + zt_s[...] + damp
    xs, ys = xl + xc, yl + yc
    ri = 1.0 / (xs + ys + zd)
    ri_s[...] = ri

    a, c, e = yl * ri, yc * ri, (xs + zd) * ri
    for n, s in enumerate(strides_of(Y)):
        a2, c2 = a * up(a, s, 1.0), c * down(c, s, 1.0)
        e2 = e + a * up(e, s, 0.0) + c * down(e, s, 0.0)
        inv = 1.0 / (a2 + c2 + e2)
        wy_s[n, 0], wy_s[n, 1], wy_s[n, 2] = inv, a * inv, c * inv
        a, c, e = a2 * inv, c2 * inv, e2 * inv
    ly_s[...], ry_s[...] = a, c
    syc[0], syc[1], syc[2], syc[3] = a[0], a[Y - 1], c[0], c[Y - 1]
    ycb[gy] = syc[...]
    for j in y_peers:
        comm.send(syc, ycb.at[gy], syco.at[gy], (gx, j))

    def y_local(r):
        for n, s in enumerate(strides_of(Y)):
            r = wy_s[n, 0] * r + wy_s[n, 1] * up(r, s, 0.0) + wy_s[n, 2] * down(r, s, 0.0)
        return r

    def z_terms(v):
        return zl_s[...] * pltpu.roll(v, 1, 1) + zt_s[...] * pltpu.roll(v, Z - 1, 1)

    def x_source(v, above, below):
        lower = jnp.concatenate([above[None], v[:-1]], axis=0)
        upper = jnp.concatenate([v[1:], below[None]], axis=0)
        return (fo_s[...] + yl_s[...] * lower + yc_s[...] * upper + z_terms(v)) * ri_s[...]

    def pack_edges(into, at, v, start):
        for j in range(Y):
            into = jnp.where(lane == start + j, v[j][:, 0:1], into)
            into = jnp.where(lane == start + Y + j, v[j][:, X - 1:], into)
        return into

    r = x_source(p_s[...], hyd[1], hyu[0])
    xl, xc, ri = xl_s[...], xc_s[...], ri_s[...]
    a, c = xl * ri, xc * ri
    e = (yl_s[...] + yc_s[...] + zd) * ri
    for n, s in enumerate(strides_of(X)):
        low, high = lane3 >= s, lane3 < X - s
        am = jnp.where(low, pltpu.roll(a, s, 2), 1.0)
        em = jnp.where(low, pltpu.roll(e, s, 2), 0.0)
        cp = jnp.where(high, pltpu.roll(c, X - s, 2), 1.0)
        ep = jnp.where(high, pltpu.roll(e, X - s, 2), 0.0)
        a2, c2 = a * am, c * cp
        e2 = e + a * em + c * ep
        inv = 1.0 / (a2 + c2 + e2)
        wa, wc = jnp.where(low, a * inv, 0.0), jnp.where(high, c * inv, 0.0)
        wx_s[n, 0], wx_s[n, 1], wx_s[n, 2] = inv, wa, wc
        r = inv * r + wa * pltpu.roll(r, s, 2) + wc * pltpu.roll(r, X - s, 2)
        a, c, e = a2 * inv, c2 * inv, e2 * inv
    g_s[...], lx_s[...], rx_s[...] = r, a, c

    def x_exchange(m, packed):
        sxb[m] = packed
        xb[m, gx] = packed
        for i in x_peers:
            comm.send(sxb.at[m], xb.at[m, gx], sx.at[m, gx], (i, gy))

    packed = pack_edges(jnp.zeros((Z, X), jnp.float32), 0, r, 0)
    packed = pack_edges(packed, 0, a, 2 * Y)
    packed = pack_edges(packed, 0, c, 4 * Y)
    x_exchange(0, packed)

    for i in x_peers:
        comm.send(cown, cbuf.at[gx, :, 3:3 + CY], sc.at[0, gx], (i, gy))
    for m in range(2):
        cbuf[gx, m, 3:3 + CY] = cown[m]
    for i in [gx] + x_peers:
        comm.send(cown.at[:, CY - 3:], cbuf.at[gx, :, 0:3], sc.at[1, gx], (i, south), has_s)
        comm.send(cown.at[:, 0:2], cbuf.at[gx, :, 3 + CY:], sc.at[2, gx], (i, north), has_n)

    for j in y_peers:
        await_recv(syc, ycb.at[j], ssem, syco.at[j], (gx, j))
    interface_factor(
        ny, gy, *[[ycb[d, m] for d in range(ny)] for m in range(4)], [syc[m] for m in range(4)],
        ytau, ysig, ybet, ytau2, ysig2, ydlt, ykk,
    )

    def slot(v, m):
        return v if m == 0 else pltpu.roll(v, X - m * Y, 1)

    def x_collect(m):
        for i in x_peers:
            await_recv(sxb.at[m], xb.at[m, i], ssem, sx.at[m, i], (i, gy))
        if m == 0:
            coefs = [[slot(xb[0, d], 2 + q) for d in range(nx)] for q in range(4)]
            own = [slot(sxb[0], 2 + q) for q in range(4)]
            interface_factor(nx, gx, *coefs, own, xtau, xsig, xbet, xtau2, xsig2, xdlt, xkk)
        gs = [xb[m, d] for d in range(nx)]
        ge = [slot(v, 1) for v in gs]
        return interface_solve(
            nx, gx, lambda d: ge[d] + xsig[d] * gs[d], lambda d: gs[d] + xsig2[d] * ge[d],
            sxb[m], slot(sxb[m], 1), xtau, xtau2, xkk,
        )

    def spread(v):
        return jnp.stack([jnp.broadcast_to(v[:, j:j + 1], (Z, X)) for j in range(Y)])

    def y_half(m):
        left, right = x_collect(m)
        left, right = spread(left), spread(right)
        v = g_s[...] + lx_s[...] * left + rx_s[...] * right
        q_s[...] = v
        before = jnp.where(lane3 == 0, left, pltpu.roll(v, 1, 2))
        after = jnp.where(lane3 == X - 1, right, pltpu.roll(v, X - 1, 2))
        r = (fo_s[...] + xl_s[...] * before + xc_s[...] * after + z_terms(v)) * ri_s[...]
        r = y_local(r)
        g_s[...] = r
        gs, ge = r[0], r[Y - 1]
        shy[m, 0] = ge + ysig[gy] * gs
        shy[m, 1] = gs + ysig2[gy] * ge
        yb[m, gy] = shy[m, 0]
        for j in y_peers:
            side = jnp.where(j > gy, 0, 1)
            comm.send(shy.at[m, side], yb.at[m, gy], sy.at[m, gy], (gx, j))
        for j in y_peers:
            await_recv(shy.at[m, 0], yb.at[m, j], ssem, sy.at[m, j], (gx, j))
        above, below = interface_solve(
            ny, gy, lambda d: yb[m, d], lambda d: yb[m, d], g_s[0], g_s[Y - 1], ytau, ytau2, ykk
        )
        return g_s[...] + ly_s[...] * above[None] + ry_s[...] * below[None], above, below

    v, above, below = y_half(0)
    r = x_source(v, above, below)
    for n, s in enumerate(strides_of(X)):
        r = wx_s[n, 0] * r + wx_s[n, 1] * pltpu.roll(r, s, 2) + wx_s[n, 2] * pltpu.roll(r, X - s, 2)
    g_s[...] = r
    x_exchange(1, pack_edges(jnp.zeros((Z, X), jnp.float32), 0, r, 0))
    v, above, below = y_half(1)

    change = v - q_s[...]
    stacked = jnp.concatenate(
        [pairs(xc_s[...] * change), pairs(xl_s[...] * change), pairs(z_terms(change))], axis=1
    )
    sel3 = jnp.concatenate([selection(1, off), selection(-1, off), here], axis=0)
    partial = mxu(stacked, sel3).reshape(CY, CZ, X)
    rown[...] = partial
    rbuf[gx, 2:2 + CY] = partial
    for i in x_peers:
        comm.send(rown, rbuf.at[gx, 2:2 + CY], sr.at[0, gx], (i, gy))
    for i in [gx] + x_peers:
        comm.send(rown.at[CY - 2:], rbuf.at[gx, 0:2], sr.at[1, gx], (i, south), has_s)
        comm.send(rown.at[0:2], rbuf.at[gx, 2 + CY:], sr.at[2, gx], (i, north), has_n)
    for j in range(Y):
        op_ref[pl.ds(j, Z, stride=Y), :] = v[j]

    for i in x_peers:
        await_recv(cown, cbuf.at[i, :, 3:3 + CY], ssem, sc.at[0, i], (i, gy))
    for i in [gx] + x_peers:
        await_recv(cown.at[:, CY - 3:], cbuf.at[i, :, 0:3], ssem, sc.at[1, i], (i, south), has_n)
        await_recv(cown.at[:, 0:2], cbuf.at[i, :, 3 + CY:], ssem, sc.at[2, i], (i, north), has_s)

    tiles = nx // 2
    first = lane3 < half
    XX = tiles * X
    wide = lax.broadcasted_iota(jnp.int32, (1, 1, XX), 2)

    def whole(m):
        near = [jnp.where(first, cbuf[2 * t, m], cbuf[2 * t + 1, m]) for t in range(tiles)]
        far = [pltpu.roll(jnp.where(first, cbuf[2 * t + 1, m], cbuf[2 * t, m]), half, 2) for t in range(tiles)]
        return jnp.concatenate(near, axis=2), jnp.concatenate(far, axis=2)

    cx, cy = whole(0)
    cz, cd = whole(1)
    czl = lax.broadcasted_iota(jnp.int32, (1, CZ, 1), 1)
    H = CY + 4
    row = lax.broadcasted_iota(jnp.int32, (H, 1, 1), 0)
    inside = jnp.logical_and(
        jnp.logical_or(row >= 2, has_n), jnp.logical_or(row < 2 + CY, has_s)
    )
    cyl, cy = cy[:H], cy[1:]
    cx, cz, cd = cx[1:], cz[1:], cd[1:]
    cd = jnp.where(inside, cd, 1.0)
    ct = jnp.where(czl < CZ - 1, cz, 0.0)
    cl = pltpu.roll(ct, 1, 1)
    cxl = jnp.where(wide == 0, 0.0, pltpu.roll(cx, 1, 2))
    diag = cxl + cx + cyl + cy + cl + ct + cd
    scale = RELAX / diag

    for i in x_peers:
        await_recv(rown, rbuf.at[i, 2:2 + CY], ssem, sr.at[0, i], (i, gy))
    for i in [gx] + x_peers:
        await_recv(rown.at[CY - 2:], rbuf.at[i, 0:2], ssem, sr.at[1, i], (i, south), has_n)
        await_recv(rown.at[0:2], rbuf.at[i, 2 + CY:], ssem, sr.at[2, i], (i, north), has_s)

    res = []
    for t in range(tiles):
        w = jnp.where(lane3 < X - 1, rbuf[2 * t], 0.0) + jnp.where(lane3 > 0, rbuf[2 * t + 1], 0.0)
        if t > 0:
            w = w + jnp.where(lane3 == 0, rbuf[2 * t - 1], 0.0)
        if t < tiles - 1:
            w = w + jnp.where(lane3 == X - 1, rbuf[2 * t + 2], 0.0)
        res.append(w)
        corr[t] = w[2:2 + CY]
    own = corr[gx // 2]
    own = jnp.where(lax.rem(gx, 2) == 0, own, pltpu.roll(own, half, 2))
    for j in range(CY):
        flip[pl.ds(j, CZ, stride=CY), :] = own[j]
    or_ref[...] = flip[0:CZ * CY, :half]
    res = jnp.concatenate(res, axis=2)
    cor = scale * res
    for repeat in range(COARSE - 1):
        lo, n = 1 + repeat, H - 2 - 2 * repeat
        cut = slice(lo, lo + n)
        mid, above, below = cor[1:-1], cor[:-2], cor[2:]
        applied = (
            diag[cut] * mid
            - cxl[cut] * pltpu.roll(mid, 1, 2)
            - cx[cut] * jnp.where(wide < XX - 1, pltpu.roll(mid, XX - 1, 2), 0.0)
            - cyl[cut] * above
            - cy[cut] * below
            - cl[cut] * pltpu.roll(mid, 1, 1)
            - ct[cut] * pltpu.roll(mid, CZ - 1, 1)
        )
        cor = jnp.where(inside[cut], mid + scale[cut] * (res[cut] - applied), 0.0)
    for j in range(CY):
        for t in range(tiles):
            flip[pl.ds((t + 1) * CZ * CY + j, CZ, stride=CY), :] = cor[j][:, t * X:(t + 1) * X]
    for t in range(tiles):
        oc_ref[:, t * X:(t + 1) * X] = flip[(t + 1) * CZ * CY:(t + 2) * CZ * CY, :]
    comm.finish()


def body(nx, ny, *args):
    Z, Y, X = args[0].shape
    CZ, CY = Z // 2, Y // 2
    flat = [v.reshape(Z * Y, X) for v in args]
    f32 = jnp.float32

    def vm(*shape):
        return pltpu.VMEM(shape, f32)

    block = (Y, Z, X)
    nsx, nsy = len(strides_of(X)), len(strides_of(Y))
    tables_x = [vm(nx, Z, X) for _ in range(6)] + [vm(6, Z, X)]
    tables_y = [vm(ny, Z, X) for _ in range(6)] + [vm(6, Z, X)]
    sends = 3 + (ny - 1) * 3 + (nx - 1) * 4 + nx * 4
    dma = pltpu.SemaphoreType.DMA
    scratch = (
        [vm(*block) for _ in range(11)]
        + [vm(*block), vm(*block), vm(nsx, 3, *block), vm(*block), vm(*block), vm(nsy, 3, *block)]
        + [vm(Z, X), vm(3, Z, X), vm(Z, X), vm(2, Z, X), vm(1, Z, X)]
        + [vm(2, nx, Z, X), vm(2, Z, X), vm(ny, 4, Z, X), vm(4, Z, X), vm(2, ny, Z, X), vm(2, 2, Z, X)]
        + tables_x + tables_y
        + [vm(CY * Z, X), vm(2, CY, CZ, X), vm(nx, 2, CY + 5, CZ, X), vm(CY, CZ, X), vm(nx, CY + 4, CZ, X),
           vm(nx // 2, CY, CZ, X), vm((nx // 2 + 1) * CZ * CY, X)]
        + [dma((sends,)), dma((3,)), dma((2, nx)), dma((ny,)), dma((2, ny)), dma((3, nx)), dma((3, nx))]
    )
    p, r, c = pl.pallas_call(
        functools.partial(kernel, nx, ny),
        out_shape=(
            jax.ShapeDtypeStruct((Z * Y, X), f32),
            jax.ShapeDtypeStruct((CZ * CY, X // 2), f32),
            jax.ShapeDtypeStruct((CZ * CY, nx * X // 2), f32),
        ),
        in_specs=[pl.BlockSpec(memory_space=pltpu.VMEM)] * 6,
        out_specs=[pl.BlockSpec(memory_space=pltpu.VMEM)] * 3,
        scratch_shapes=scratch,
        compiler_params=pltpu.CompilerParams(
            collective_id=0, has_side_effects=True, vmem_limit_bytes=48 * 1024 * 1024
        ),
    )(*flat)
    return p.reshape(Z, Y, X), r.reshape(CZ, CY, X // 2), c.reshape(CZ, CY, nx * X // 2)


def solution(mesh):
    nx, ny = mesh.shape["gx"], mesh.shape["gy"]
    split = P(None, "gy", "gx")
    return jax.shard_map(
        functools.partial(body, nx, ny),
        mesh=mesh,
        in_specs=(split,) * 6,
        out_specs=(split, split, P(None, "gy", None)),
        check_vma=False,
    )
```

time: 387 us -> 43.4 us (0.11)
  blocking collectives: 113 us -> 0 us
  starting transfers between devices: 107 us -> 0 us
  local copies, waits for them, and re-layouts: 77.1 us -> 7.32 us
  other arithmetic: 45.6 us -> 0 us
  waiting for transfers between devices: 37.7 us -> 0 us
  Pallas kernels: 0 us -> 35.2 us
    all_gather x5 -> x0, blocking collectives: 103 us -> none  [the longest x1 21.4 us: body(): lax.all_gather(coarse_residual, 'gx', axis=2, tiled=True)]
    ppermute x19 -> x0, starting transfers between devices: 53.7 us -> none  [the longest x8 26.9 us: extended(): before = lax.ppermute(last, axis, up)]
    all_to_all x11 -> x0, starting transfers between devices: 53.6 us -> none  [the longest x2 12.6 us: body(): lax.all_to_all(source, 'gy', split_axis=0, concat_axis=1, tiled=True)]
    reshape x5 -> x0, local copies, waits for them, and re-layouts: 48.6 us -> none  [restrict(): blocks = field.reshape(levels // 2, 2, rows // 2, 2, columns // 2, 2)]
    pallas_call x0 -> x1, Pallas kernels: none -> 35.2 us  [body(): pl.pallas_call(functools.partial(kernel, nx, ny), out_shape=(jax.ShapeDty...]
    reduce_sum x5 -> x0, other arithmetic: 22 us -> none  [restrict(): return jnp.sum(blocks, axis=(1, 3, 5)) * 0.125]
    ppermute x19 -> x0, waiting for transfers between devices: 19.6 us -> none  [the longest x8 14.6 us: extended(): after = lax.ppermute(leading, axis, down)]
    all_to_all x11 -> x0, waiting for transfers between devices: 18.1 us -> none  [the longest x2 7.71 us: body(): lax.all_to_all(source, 'gy', split_axis=0, concat_axis=1, tiled=True)]
  transfers between devices with their start and end apart: 30 -> 0, of which waited for: 15 -> 0; matrix products, arithmetic and copies ran while one was open for 26% -> 0% of each run, Pallas kernels for 0% -> 0%
where the time goes in v1:
time: 43.4 us; the launch traced here: 43.1 us
  Pallas kernels  35.2 us (81%)
  local copies, waits for them, and re-layouts  7.32 us (17%)
  between operations  0.65 us (1%)
    pallas_call x1, Pallas kernels, body(): pl.pallas_call(functools.partial(kernel, nx, ny), out_shape=(jax.ShapeDty...  35.2 us
    unnamed x15, local copies, waits for them, and re-layouts  7.32 us

profile of v1, /device:TPU:1, one launch (start us, length us, event | category | flops | bytes accessed | tf_op | source)
XLA Modules:
  0.0 43.1 jit_solution(16081041491587162919)
XLA Ops:
  0.6 0.0 copy-start
  0.6 0.9 %copy-done = f32[16,16,128]{2,1,0:T(8,128)S(1)} copy-done((f32[16,16,128]{2,1,0:T(8,128)S(1)}, f32[16,16,128]{2,1,0:T(8,128)}, u32[]{:S(2)}) %copy-start) | copy-done | bytes 131096
  1.5 0.0 copy-start.1
  1.5 0.9 %copy-done.1 = f32[16,16,128]{2,1,0:T(8,128)S(1)} copy-done((f32[16,16,128]{2,1,0:T(8,128)S(1)}, f32[16,16,128]{2,1,0:T(8,128)}, u32[]{:S(2)}) %copy-start.1) | copy-done | bytes 131096
  2.4 0.0 copy-start.2
  2.4 0.9 %copy-done.2 = f32[16,16,128]{2,1,0:T(8,128)S(1)} copy-done((f32[16,16,128]{2,1,0:T(8,128)S(1)}, f32[16,16,128]{2,1,0:T(8,128)}, u32[]{:S(2)}) %copy-start.2) | copy-done | bytes 131096
  3.3 0.0 copy-start.3
  3.3 0.9 %copy-done.3 = f32[16,16,128]{2,1,0:T(8,128)S(1)} copy-done((f32[16,16,128]{2,1,0:T(8,128)S(1)}, f32[16,16,128]{2,1,0:T(8,128)}, u32[]{:S(2)}) %copy-start.3) | copy-done | bytes 131096
  4.3 0.0 copy-start.4
  4.3 0.9 %copy-done.4 = f32[16,16,128]{2,1,0:T(8,128)S(1)} copy-done((f32[16,16,128]{2,1,0:T(8,128)S(1)}, f32[16,16,128]{2,1,0:T(8,128)}, u32[]{:S(2)}) %copy-start.4) | copy-done | bytes 131096
  5.2 0.0 copy-start.5
  5.2 0.9 %copy-done.5 = f32[16,16,128]{2,1,0:T(8,128)S(1)} copy-done((f32[16,16,128]{2,1,0:T(8,128)S(1)}, f32[16,16,128]{2,1,0:T(8,128)}, u32[]{:S(2)}) %copy-start.5) | copy-done | bytes 131096
  6.1 35.2 %shard_map.85 = (f32[256,128]{1,0:T(8,128)S(1)}, f32[64,64]{1,0:T(8,128)S(1)}, f32[64,256]{1,0:T(8,128)S(1)}) custom-call(f32[256,128]{1,0:T(8,128)S(1)} %bitcast.10, f32[256,128]{1,0:T(8,128)S(1)} %bitcast.11, f32[256,128]{1,0:T(8,128)S(1)} %bitcast.12, f32[256,128]{1,0:T(8,128)S(1)} %bitcast.13, f32[256,128]{1,0:T(8,128)S(1)} %bitcast.14, ...), custom_call_target="tpu_custom_call" | custom-call | tf_op jit(solution)/shard_map/pallas_call | solution.py:479
  41.2 0.7 %copy.12 = f32[16,16,128]{2,1,0:T(8,128)} copy(f32[16,16,128]{2,1,0:T(8,128)S(1)} %bitcast.9) | data formatting | bytes 262144
  41.9 0.6 %copy.13 = f32[8,8,64]{2,1,0:T(8,128)} copy(f32[8,8,64]{2,1,0:T(8,128)S(1)} %bitcast.17) | data formatting | bytes 32768
  42.5 0.6 %copy.14 = f32[8,8,256]{2,1,0:T(8,128)} copy(f32[8,8,256]{2,1,0:T(8,128)S(1)} %bitcast.16) | data formatting | bytes 131072
Async XLA Ops:
  0.6 0.9 %copy-start = (f32[16,16,128]{2,1,0:T(8,128)S(1)}, f32[16,16,128]{2,1,0:T(8,128)}, u32[]{:S(2)}) copy-start(f32[16,16,128]{2,1,0:T(8,128)} %param.6) | copy-start | bytes 393220
  1.5 0.9 %copy-start.1 = (f32[16,16,128]{2,1,0:T(8,128)S(1)}, f32[16,16,128]{2,1,0:T(8,128)}, u32[]{:S(2)}) copy-start(f32[16,16,128]{2,1,0:T(8,128)} %param.7) | copy-start | bytes 393220
  2.4 0.9 %copy-start.2 = (f32[16,16,128]{2,1,0:T(8,128)S(1)}, f32[16,16,128]{2,1,0:T(8,128)}, u32[]{:S(2)}) copy-start(f32[16,16,128]{2,1,0:T(8,128)} %param.8) | copy-start | bytes 393220
  3.3 0.9 %copy-start.3 = (f32[16,16,128]{2,1,0:T(8,128)S(1)}, f32[16,16,128]{2,1,0:T(8,128)}, u32[]{:S(2)}) copy-start(f32[16,16,128]{2,1,0:T(8,128)} %param.9) | copy-start | bytes 393220
  4.3 0.9 %copy-start.4 = (f32[16,16,128]{2,1,0:T(8,128)S(1)}, f32[16,16,128]{2,1,0:T(8,128)}, u32[]{:S(2)}) copy-start(f32[16,16,128]{2,1,0:T(8,128)} %param.10) | copy-start | bytes 393220
  5.2 0.9 %copy-start.5 = (f32[16,16,128]{2,1,0:T(8,128)S(1)}, f32[16,16,128]{2,1,0:T(8,128)}, u32[]{:S(2)}) copy-start(f32[16,16,128]{2,1,0:T(8,128)} %param.11) | copy-start | bytes 393220

commit v2 on v1

--- a/solution.py
+++ b/solution.py
@@ -102,14 +102,14 @@
     return kk[0] * p + kk[1] * q, kk[2] * q + kk[3] * p
 
 
-def kernel(nx, ny, f_ref, p_ref, x_ref, y_ref, z_ref, d_ref, op_ref, or_ref, oc_ref,
+def kernel(nx, ny, f_hbm, p_hbm, x_hbm, y_hbm, z_hbm, d_hbm, op_ref, or_ref, oc_ref,
            xl_s, xc_s, yl_s, yc_s, zl_s, zt_s, fo_s, p_s, ri_s, g_s, q_s,
            lx_s, rx_s, wx_s, ly_s, ry_s, wy_s,
            sx0, sy0, hx, hyd, hyu, xb, sxb, ycb, syc, yb, shy,
            xtau, xsig, xbet, xtau2, xsig2, xdlt, xkk,
            ytau, ysig, ybet, ytau2, ysig2, ydlt, ykk,
-           pair_s, cown, cbuf, rown, rbuf, corr, flip,
-           ssem, s0, sx, syco, sy, sc, sr):
+           pair_s, cown, cbuf, rown, rbuf, fown, fbuf, flip,
+           ssem, s0, sx, syco, sy, sc, sr, sf, ins, sin):
     Y, Z, X = xc_s.shape
     CY, CZ = Y // 2, Z // 2
     gx, gy = lax.axis_index("gx"), lax.axis_index("gy")
@@ -120,6 +120,12 @@
     x_peers = [lax.rem(gx + o, nx) for o in range(1, nx)]
     y_peers = [lax.rem(gy + o, ny) for o in range(1, ny)]
 
+    loads = []
+    for m, ref in enumerate((x_hbm, y_hbm, p_hbm, z_hbm, d_hbm, f_hbm)):
+        loads.append(pltpu.make_async_copy(ref, ins.at[m], sin.at[m]))
+        loads[m].start()
+    x_ref, y_ref, p_ref, z_ref, d_ref, f_ref = [ins.at[m] for m in range(6)]
+
     barrier = pltpu.get_barrier_semaphore()
 
     def greet(dev):
@@ -130,15 +136,11 @@
     for j in y_peers:
         greet((gx, j))
 
-    @pl.when(has_n)
-    def _():
-        for i in x_peers:
-            greet((i, north))
-
-    @pl.when(has_s)
-    def _():
-        for i in x_peers:
-            greet((i, south))
+    corners = [
+        (jnp.logical_and(h, v), (i, j)) for h, i in ((has_w, west), (has_e, east)) for v, j in ((has_n, north), (has_s, south))
+    ]
+    for cond, dev in corners:
+        pl.when(cond)(functools.partial(greet, dev))
 
     lane = lax.broadcasted_iota(jnp.int32, (Z, X), 1)
     level = lax.broadcasted_iota(jnp.int32, (Z, X), 0)
@@ -148,16 +150,21 @@
         return ref[pl.ds(j, Z, stride=Y), :]
 
     packed = jnp.zeros((Z, X), jnp.float32)
+    for m in range(3):
+        loads[m].wait()
     for j in range(Y):
         v = rows(x_ref, j)
         xc_s[j] = v
         packed = jnp.where(lane == j, v[:, X - 1:], packed)
         yc_s[j] = rows(y_ref, j)
+        p_s[j] = rows(p_ref, j)
+    for m in range(3, 6):
+        loads[m].wait()
+    for j in range(Y):
         zv = jnp.where(level < Z - 1, rows(z_ref, j), 0.0)
         zt_s[j] = zv
         zl_s[j] = pltpu.roll(zv, 1, 0)
         fo_s[j] = rows(f_ref, j)
-        p_s[j] = rows(p_ref, j)
     sx0[...] = packed
     sy0[0] = yc_s[Y - 1]
     sy0[1] = p_s[Y - 1]
@@ -166,23 +173,30 @@
     @pl.when(jnp.logical_not(has_w))
     def _():
         hx[...] = jnp.zeros_like(hx)
+        cbuf[0] = jnp.zeros_like(cbuf[0])
+        rbuf[0] = jnp.zeros_like(rbuf[0])
+
+    @pl.when(jnp.logical_not(has_e))
+    def _():
+        cbuf[2] = jnp.zeros_like(cbuf[2])
+        rbuf[2] = jnp.zeros_like(rbuf[2])
 
     @pl.when(jnp.logical_not(has_n))
     def _():
         hyd[...] = jnp.zeros_like(hyd)
-        for d in range(nx):
+        for d in range(3):
             cbuf[d, :, 0:3] = jnp.zeros_like(cbuf[d, :, 0:3])
             rbuf[d, 0:2] = jnp.zeros_like(rbuf[d, 0:2])
 
     @pl.when(jnp.logical_not(has_s))
     def _():
         hyu[...] = jnp.zeros_like(hyu)
-        for d in range(nx):
+        for d in range(3):
             cbuf[d, :, 3 + CY:] = jnp.zeros_like(cbuf[d, :, 3 + CY:])
             rbuf[d, 2 + CY:] = jnp.zeros_like(rbuf[d, 2 + CY:])
 
-    both = has_n.astype(jnp.int32) + has_s.astype(jnp.int32)
-    pl.semaphore_wait(barrier, (nx - 1) + (ny - 1) + (nx - 1) * both)
+    n_corners = sum(cond.astype(jnp.int32) for cond, _ in corners)
+    pl.semaphore_wait(barrier, (nx - 1) + (ny - 1) + n_corners)
 
     comm = Comm(ssem)
     comm.send(sx0, hx, s0.at[0], (east, gy), has_e)
@@ -190,7 +204,7 @@
     comm.send(sy0.at[2:3], hyu, s0.at[2], (gx, north), has_n)
 
     half = X // 2
-    off = lax.rem(gx, 2) * half
+    off = half // 2
     ii = lax.broadcasted_iota(jnp.int32, (X, X), 0)
     mm = lax.broadcasted_iota(jnp.int32, (X, X), 1)
 
@@ -206,7 +220,7 @@
     def mxu(a, b):
         return jnp.dot(a, b, precision=lax.Precision.HIGHEST, preferred_element_type=jnp.float32)
 
-    here, there = selection(0, off), selection(0, half - off)
+    here, there = selection(0, off), selection(0, half + off)
     sel2 = jnp.concatenate([here, there], axis=0)
     zfull = jnp.stack([rows(z_ref, j) for j in range(Y)])
     damp = jnp.stack([rows(d_ref, j) for j in range(Y)])
@@ -291,13 +305,29 @@
     packed = pack_edges(packed, 0, c, 4 * Y)
     x_exchange(0, packed)
 
-    for i in x_peers:
-        comm.send(cown, cbuf.at[gx, :, 3:3 + CY], sc.at[0, gx], (i, gy))
+    def halo_exchange(src, dst, sems, top, lead, starting):
+        def part(ref, lo, n):
+            return ref.at[(slice(None),) * lead + (pl.ds(lo, n),)]
+
+        def rows_of(slot):
+            return dst.at[slot]
+
+        for slot, i, ok, back in ((0, west, has_w, 2), (1, gx, None, 1), (2, east, has_e, 0)):
+            both_ok = (lambda c: c) if ok is None else (lambda c, ok=ok: jnp.logical_and(c, ok))
+            if starting:
+                if ok is not None:
+                    comm.send(src, part(rows_of(back), top, CY), sems.at[0, back], (i, gy), ok)
+                comm.send(part(src, CY - top, top), part(rows_of(back), 0, top), sems.at[1, back], (i, south), both_ok(has_s))
+                comm.send(part(src, 0, 2), part(rows_of(back), top + CY, 2), sems.at[2, back], (i, north), both_ok(has_n))
+            else:
+                if ok is not None:
+                    await_recv(src, part(rows_of(slot), top, CY), ssem, sems.at[0, slot], (i, gy), ok)
+                await_recv(part(src, CY - top, top), part(rows_of(slot), 0, top), ssem, sems.at[1, slot], (i, south), both_ok(has_n))
+                await_recv(part(src, 0, 2), part(rows_of(slot), top + CY, 2), ssem, sems.at[2, slot], (i, north), both_ok(has_s))
+
     for m in range(2):
-        cbuf[gx, m, 3:3 + CY] = cown[m]
-    for i in [gx] + x_peers:
-        comm.send(cown.at[:, CY - 3:], cbuf.at[gx, :, 0:3], sc.at[1, gx], (i, south), has_s)
-        comm.send(cown.at[:, 0:2], cbuf.at[gx, :, 3 + CY:], sc.at[2, gx], (i, north), has_n)
+        cbuf[1, m, 3:3 + CY] = cown[m]
+    halo_exchange(cown, cbuf, sc, 3, 1, True)
 
     for j in y_peers:
         await_recv(syc, ycb.at[j], ssem, syco.at[j], (gx, j))
@@ -365,69 +395,51 @@
     sel3 = jnp.concatenate([selection(1, off), selection(-1, off), here], axis=0)
     partial = mxu(stacked, sel3).reshape(CY, CZ, X)
     rown[...] = partial
-    rbuf[gx, 2:2 + CY] = partial
-    for i in x_peers:
-        comm.send(rown, rbuf.at[gx, 2:2 + CY], sr.at[0, gx], (i, gy))
-    for i in [gx] + x_peers:
-        comm.send(rown.at[CY - 2:], rbuf.at[gx, 0:2], sr.at[1, gx], (i, south), has_s)
-        comm.send(rown.at[0:2], rbuf.at[gx, 2 + CY:], sr.at[2, gx], (i, north), has_n)
+    rbuf[1, 2:2 + CY] = partial
+    halo_exchange(rown, rbuf, sr, 2, 0, True)
     for j in range(Y):
         op_ref[pl.ds(j, Z, stride=Y), :] = v[j]
 
-    for i in x_peers:
-        await_recv(cown, cbuf.at[i, :, 3:3 + CY], ssem, sc.at[0, i], (i, gy))
-    for i in [gx] + x_peers:
-        await_recv(cown.at[:, CY - 3:], cbuf.at[i, :, 0:3], ssem, sc.at[1, i], (i, south), has_n)
-        await_recv(cown.at[:, 0:2], cbuf.at[i, :, 3 + CY:], ssem, sc.at[2, i], (i, north), has_s)
-
-    tiles = nx // 2
-    first = lane3 < half
-    XX = tiles * X
-    wide = lax.broadcasted_iota(jnp.int32, (1, 1, XX), 2)
-
-    def whole(m):
-        near = [jnp.where(first, cbuf[2 * t, m], cbuf[2 * t + 1, m]) for t in range(tiles)]
-        far = [pltpu.roll(jnp.where(first, cbuf[2 * t + 1, m], cbuf[2 * t, m]), half, 2) for t in range(tiles)]
-        return jnp.concatenate(near, axis=2), jnp.concatenate(far, axis=2)
-
-    cx, cy = whole(0)
-    cz, cd = whole(1)
+    halo_exchange(cown, cbuf, sc, 3, 1, False)
+
+    centre = jnp.logical_and(lane3 >= off, lane3 < off + half)
+    wide = lane3
+
+    def planes(m):
+        w, o, e = cbuf[0, m], cbuf[1, m], cbuf[2, m]
+        near = jnp.where(centre, o, pltpu.roll(jnp.where(lane3 >= half, w, e), half, 2))
+        far = jnp.where(centre, pltpu.roll(o, half, 2), jnp.where(lane3 < half, w, e))
+        return near, far
+
+    cx, cy = planes(0)
+    cz, cd = planes(1)
     czl = lax.broadcasted_iota(jnp.int32, (1, CZ, 1), 1)
     H = CY + 4
     row = lax.broadcasted_iota(jnp.int32, (H, 1, 1), 0)
     inside = jnp.logical_and(
         jnp.logical_or(row >= 2, has_n), jnp.logical_or(row < 2 + CY, has_s)
     )
+    inside = jnp.logical_and(
+        inside,
+        jnp.logical_and(jnp.logical_or(lane3 >= off, has_w), jnp.logical_or(lane3 < off + half, has_e)),
+    )
     cyl, cy = cy[:H], cy[1:]
     cx, cz, cd = cx[1:], cz[1:], cd[1:]
     cd = jnp.where(inside, cd, 1.0)
     ct = jnp.where(czl < CZ - 1, cz, 0.0)
     cl = pltpu.roll(ct, 1, 1)
-    cxl = jnp.where(wide == 0, 0.0, pltpu.roll(cx, 1, 2))
+    cxl = pltpu.roll(cx, 1, 2)
     diag = cxl + cx + cyl + cy + cl + ct + cd
     scale = RELAX / diag
 
-    for i in x_peers:
-        await_recv(rown, rbuf.at[i, 2:2 + CY], ssem, sr.at[0, i], (i, gy))
-    for i in [gx] + x_peers:
-        await_recv(rown.at[CY - 2:], rbuf.at[i, 0:2], ssem, sr.at[1, i], (i, south), has_n)
-        await_recv(rown.at[0:2], rbuf.at[i, 2 + CY:], ssem, sr.at[2, i], (i, north), has_s)
-
-    res = []
-    for t in range(tiles):
-        w = jnp.where(lane3 < X - 1, rbuf[2 * t], 0.0) + jnp.where(lane3 > 0, rbuf[2 * t + 1], 0.0)
-        if t > 0:
-            w = w + jnp.where(lane3 == 0, rbuf[2 * t - 1], 0.0)
-        if t < tiles - 1:
-            w = w + jnp.where(lane3 == X - 1, rbuf[2 * t + 2], 0.0)
-        res.append(w)
-        corr[t] = w[2:2 + CY]
-    own = corr[gx // 2]
-    own = jnp.where(lax.rem(gx, 2) == 0, own, pltpu.roll(own, half, 2))
-    for j in range(CY):
-        flip[pl.ds(j, CZ, stride=CY), :] = own[j]
-    or_ref[...] = flip[0:CZ * CY, :half]
-    res = jnp.concatenate(res, axis=2)
+    halo_exchange(rown, rbuf, sr, 2, 0, False)
+    w, e = pltpu.roll(rbuf[0], half, 2), pltpu.roll(rbuf[2], half, 2)
+    res = (
+        rbuf[1]
+        + jnp.where(jnp.logical_and(lane3 >= off - 2, lane3 <= off), w, 0.0)
+        + jnp.where(jnp.logical_and(lane3 >= off + half - 1, lane3 <= off + half + 1), e, 0.0)
+    )
+    res = jnp.where(inside, res, 0.0)
     cor = scale * res
     for repeat in range(COARSE - 1):
         lo, n = 1 + repeat, H - 2 - 2 * repeat
@@ -436,19 +448,43 @@
         applied = (
             diag[cut] * mid
             - cxl[cut] * pltpu.roll(mid, 1, 2)
-            - cx[cut] * jnp.where(wide < XX - 1, pltpu.roll(mid, XX - 1, 2), 0.0)
+            - cx[cut] * pltpu.roll(mid, X - 1, 2)
             - cyl[cut] * above
             - cy[cut] * below
             - cl[cut] * pltpu.roll(mid, 1, 1)
             - ct[cut] * pltpu.roll(mid, CZ - 1, 1)
         )
         cor = jnp.where(inside[cut], mid + scale[cut] * (res[cut] - applied), 0.0)
+    hj = CY // 2
+    mine = jnp.where(lane3 < half, pltpu.roll(cor[:hj], X - off, 2), pltpu.roll(cor[hj:], off, 2))
+    fown[...] = mine
+    fbuf[gx] = mine
+    for i in x_peers:
+        comm.send(fown, fbuf.at[gx], sf.at[gx], (i, gy))
+    own = pltpu.roll(res[2:2 + CY], X - off, 2)
     for j in range(CY):
-        for t in range(tiles):
-            flip[pl.ds((t + 1) * CZ * CY + j, CZ, stride=CY), :] = cor[j][:, t * X:(t + 1) * X]
-    for t in range(tiles):
-        oc_ref[:, t * X:(t + 1) * X] = flip[(t + 1) * CZ * CY:(t + 2) * CZ * CY, :]
+        flip[pl.ds(j, CZ, stride=CY), :] = own[j]
+    or_ref[...] = flip[0:CZ * CY, :half]
+    for i in x_peers:
+        await_recv(fown, fbuf.at[i], ssem, sf.at[i], (i, gy))
+    for t in range(nx // 2):
+        u, v = fbuf[2 * t], fbuf[2 * t + 1]
+        top = jnp.where(lane3 < half, u, pltpu.roll(v, half, 2))
+        low = jnp.where(lane3 < half, pltpu.roll(u, half, 2), v)
+        base = (t + 1) * CZ * CY
+        for j in range(CY):
+            flip[pl.ds(base + j, CZ, stride=CY), :] = top[j] if j < hj else low[j - hj]
+        oc_ref[:, t * X:(t + 1) * X] = flip[base:base + CZ * CY, :]
     comm.finish()
+
+
+def put(*refs):
+    sems = refs[6]
+    copies = [pltpu.make_async_copy(refs[m], refs[3 + m], sems.at[m]) for m in range(3)]
+    for copy in copies:
+        copy.start()
+    for copy in copies:
+        copy.wait()
 
 
 def body(nx, ny, *args):
@@ -464,7 +500,7 @@
     nsx, nsy = len(strides_of(X)), len(strides_of(Y))
     tables_x = [vm(nx, Z, X) for _ in range(6)] + [vm(6, Z, X)]
     tables_y = [vm(ny, Z, X) for _ in range(6)] + [vm(6, Z, X)]
-    sends = 3 + (ny - 1) * 3 + (nx - 1) * 4 + nx * 4
+    sends = 3 + (ny - 1) * 3 + (nx - 1) * 3 + 8 * 2
     dma = pltpu.SemaphoreType.DMA
     scratch = (
         [vm(*block) for _ in range(11)]
@@ -472,9 +508,10 @@
         + [vm(Z, X), vm(3, Z, X), vm(Z, X), vm(2, Z, X), vm(1, Z, X)]
         + [vm(2, nx, Z, X), vm(2, Z, X), vm(ny, 4, Z, X), vm(4, Z, X), vm(2, ny, Z, X), vm(2, 2, Z, X)]
         + tables_x + tables_y
-        + [vm(CY * Z, X), vm(2, CY, CZ, X), vm(nx, 2, CY + 5, CZ, X), vm(CY, CZ, X), vm(nx, CY + 4, CZ, X),
-           vm(nx // 2, CY, CZ, X), vm((nx // 2 + 1) * CZ * CY, X)]
-        + [dma((sends,)), dma((3,)), dma((2, nx)), dma((ny,)), dma((2, ny)), dma((3, nx)), dma((3, nx))]
+        + [vm(CY * Z, X), vm(2, CY, CZ, X), vm(3, 2, CY + 5, CZ, X), vm(CY, CZ, X), vm(3, CY + 4, CZ, X),
+           vm(CY // 2, CZ, X), vm(nx, CY // 2, CZ, X), vm((nx // 2 + 1) * CZ * CY, X)]
+        + [dma((sends,)), dma((3,)), dma((2, nx)), dma((ny,)), dma((2, ny)), dma((3, 3)), dma((3, 3)), dma((nx,))]
+        + [vm(6, Z * Y, X), dma((6,))]
     )
     p, r, c = pl.pallas_call(
         functools.partial(kernel, nx, ny),
@@ -483,11 +520,11 @@
             jax.ShapeDtypeStruct((CZ * CY, X // 2), f32),
             jax.ShapeDtypeStruct((CZ * CY, nx * X // 2), f32),
         ),
-        in_specs=[pl.BlockSpec(memory_space=pltpu.VMEM)] * 6,
+        in_specs=[pl.BlockSpec(memory_space=pltpu.HBM)] * 6,
         out_specs=[pl.BlockSpec(memory_space=pltpu.VMEM)] * 3,
         scratch_shapes=scratch,
         compiler_params=pltpu.CompilerParams(
-            collective_id=0, has_side_effects=True, vmem_limit_bytes=48 * 1024 * 1024
+            collective_id=0, has_side_effects=True, vmem_limit_bytes=67043328
         ),
     )(*flat)
     return p.reshape(Z, Y, X), r.reshape(CZ, CY, X // 2), c.reshape(CZ, CY, nx * X // 2)

time: 43.4 us -> 39.1 us (0.901)
  local copies, waits for them, and re-layouts: 7.32 us -> 3.06 us
    unnamed x15 -> x7, local copies, waits for them, and re-layouts: 7.32 us -> 3.06 us
where the time goes in v2:
time: 39.1 us; the launch traced here: 38.5 us
  Pallas kernels  34.8 us (89%)
  local copies, waits for them, and re-layouts  3.06 us (8%)
  between operations  0.65 us (2%)
    pallas_call x1, Pallas kernels, body(): pl.pallas_call(functools.partial(kernel, nx, ny), out_shape=(jax.ShapeDty...  34.8 us
    unnamed x7, local copies, waits for them, and re-layouts  3.06 us

profile of v2, /device:TPU:1, one launch (start us, length us, event | category | flops | bytes accessed | tf_op | source)
XLA Modules:
  0.0 38.5 jit_solution(2962771485547116228)
XLA Ops:
  0.6 34.8 %shard_map.85 = (f32[256,128]{1,0:T(8,128)}, f32[64,64]{1,0:T(8,128)}, f32[64,256]{1,0:T(8,128)}) custom-call(f32[256,128]{1,0:T(8,128)} %bitcast.10, f32[256,128]{1,0:T(8,128)} %bitcast.11, f32[256,128]{1,0:T(8,128)} %bitcast.12, f32[256,128]{1,0:T(8,128)} %bitcast.13, f32[256,128]{1,0:T(8,128)} %bitcast.14, f32[256,128]{1,0:T(8,128)} %bitcast.15), custom_call_target="tpu_custom_call" | custom-call | tf_op jit(solution)/shard_map/pallas_call | solution.py:516
  35.4 0.0 copy-start.1
  35.5 1.6 %copy.12 = f32[16,16,128]{2,1,0:T(8,128)} copy(f32[16,16,128]{2,1,0:T(8,128)} %bitcast.9) | data formatting | bytes 262144
  37.0 0.0 copy-done.1
  37.0 0.0 copy-start
  37.0 0.6 %copy.13 = f32[8,8,64]{2,1,0:T(8,128)} copy(f32[8,8,64]{2,1,0:T(8,128)S(1)} %bitcast.17) | data formatting | bytes 32768
  37.6 0.2 copy-done
  37.9 0.6 %copy.14 = f32[8,8,256]{2,1,0:T(8,128)} copy(f32[8,8,256]{2,1,0:T(8,128)S(1)} %bitcast.16) | data formatting | bytes 131072
Async XLA Ops:
  35.4 1.6 %copy-start.1 = (f32[64,64]{1,0:T(8,128)S(1)}, f32[64,64]{1,0:T(8,128)}, u32[]{:S(2)}) copy-start(f32[64,64]{1,0:T(8,128)} %get-tuple-element.7) | copy-start | bytes 49156
  37.0 0.9 %copy-start = (f32[64,256]{1,0:T(8,128)S(1)}, f32[64,256]{1,0:T(8,128)}, u32[]{:S(2)}) copy-start(f32[64,256]{1,0:T(8,128)} %get-tuple-element.8) | copy-start | bytes 196612

commit v3 on v2

--- a/solution.py
+++ b/solution.py
@@ -9,6 +9,8 @@
 
 COARSE = 3
 RELAX = 0.8
+CH = 16
+CH2 = 4
 MESH = pl.DeviceIdType.MESH
 
 
@@ -102,14 +104,14 @@
     return kk[0] * p + kk[1] * q, kk[2] * q + kk[3] * p
 
 
-def kernel(nx, ny, f_hbm, p_hbm, x_hbm, y_hbm, z_hbm, d_hbm, op_ref, or_ref, oc_ref,
-           xl_s, xc_s, yl_s, yc_s, zl_s, zt_s, fo_s, p_s, ri_s, g_s, q_s,
+def kernel(nx, ny, f_hbm, p_hbm, x_hbm, y_hbm, z_hbm, d_hbm, op_hbm, or_hbm, oc_hbm,
+           xl_s, xc_s, yl_s, yc_s, zl_s, zt_s, fo_s, p_s, ri_s, g_s, q_s, zds_s,
            lx_s, rx_s, wx_s, ly_s, ry_s, wy_s,
            sx0, sy0, hx, hyd, hyu, xb, sxb, ycb, syc, yb, shy,
            xtau, xsig, xbet, xtau2, xsig2, xdlt, xkk,
            ytau, ysig, ybet, ytau2, ysig2, ydlt, ykk,
            pair_s, cown, cbuf, rown, rbuf, fown, fbuf, flip,
-           ssem, s0, sx, syco, sy, sc, sr, sf, ins, sin):
+           ssem, s0, sx, syco, sy, sc, sr, sf, ins, sin, op_ref, or_ref, oc_ref, sout):
     Y, Z, X = xc_s.shape
     CY, CZ = Y // 2, Z // 2
     gx, gy = lax.axis_index("gx"), lax.axis_index("gy")
@@ -270,29 +272,33 @@
         return (fo_s[...] + yl_s[...] * lower + yc_s[...] * upper + z_terms(v)) * ri_s[...]
 
     def pack_edges(into, at, v, start):
-        for j in range(Y):
-            into = jnp.where(lane == start + j, v[j][:, 0:1], into)
-            into = jnp.where(lane == start + Y + j, v[j][:, X - 1:], into)
+        for j in range(v.shape[0]):
+            into = jnp.where(lane == start + at + j, v[j][:, 0:1], into)
+            into = jnp.where(lane == start + at + Y + j, v[j][:, X - 1:], into)
         return into
 
-    r = x_source(p_s[...], hyd[1], hyu[0])
-    xl, xc, ri = xl_s[...], xc_s[...], ri_s[...]
-    a, c = xl * ri, xc * ri
-    e = (yl_s[...] + yc_s[...] + zd) * ri
-    for n, s in enumerate(strides_of(X)):
-        low, high = lane3 >= s, lane3 < X - s
-        am = jnp.where(low, pltpu.roll(a, s, 2), 1.0)
-        em = jnp.where(low, pltpu.roll(e, s, 2), 0.0)
-        cp = jnp.where(high, pltpu.roll(c, X - s, 2), 1.0)
-        ep = jnp.where(high, pltpu.roll(e, X - s, 2), 0.0)
-        a2, c2 = a * am, c * cp
-        e2 = e + a * em + c * ep
-        inv = 1.0 / (a2 + c2 + e2)
-        wa, wc = jnp.where(low, a * inv, 0.0), jnp.where(high, c * inv, 0.0)
-        wx_s[n, 0], wx_s[n, 1], wx_s[n, 2] = inv, wa, wc
-        r = inv * r + wa * pltpu.roll(r, s, 2) + wc * pltpu.roll(r, X - s, 2)
-        a, c, e = a2 * inv, c2 * inv, e2 * inv
-    g_s[...], lx_s[...], rx_s[...] = r, a, c
+    ones = jnp.ones((1, 1, X), jnp.float32)
+    packed = jnp.zeros((Z, X), jnp.float32)
+    zds_s[...] = (yl + yc + zd) * ri
+    g_s[...] = x_source(p_s[...], hyd[1], hyu[0])
+    for lo in range(0, Y, CH):
+        part = slice(lo, lo + CH)
+        a, c = xl_s[part] * ri_s[part], xc_s[part] * ri_s[part]
+        e, r = zds_s[part], g_s[part]
+        for n, s in enumerate(strides_of(X)):
+            low, high = lane3 >= s, lane3 < X - s
+            a_in, c_in = jnp.where(low, a, 0.0), jnp.where(high, c, 0.0)
+            a2 = a * jnp.where(low, pltpu.roll(a, s, 2), ones)
+            c2 = c * jnp.where(high, pltpu.roll(c, X - s, 2), ones)
+            e2 = e + a_in * pltpu.roll(e, s, 2) + c_in * pltpu.roll(e, X - s, 2)
+            inv = 1.0 / (a2 + c2 + e2)
+            wa, wc = a_in * inv, c_in * inv
+            wx_s[n, 0, part], wx_s[n, 1, part], wx_s[n, 2, part] = inv, wa, wc
+            r = inv * r + wa * pltpu.roll(r, s, 2) + wc * pltpu.roll(r, X - s, 2)
+            a, c, e = a2 * inv, c2 * inv, e2 * inv
+        g_s[part], lx_s[part], rx_s[part] = r, a, c
+        for q, v in enumerate((r, a, c)):
+            packed = pack_edges(packed, lo, v, 2 * q * Y)
 
     def x_exchange(m, packed):
         sxb[m] = packed
@@ -300,9 +306,6 @@
         for i in x_peers:
             comm.send(sxb.at[m], xb.at[m, gx], sx.at[m, gx], (i, gy))
 
-    packed = pack_edges(jnp.zeros((Z, X), jnp.float32), 0, r, 0)
-    packed = pack_edges(packed, 0, a, 2 * Y)
-    packed = pack_edges(packed, 0, c, 4 * Y)
     x_exchange(0, packed)
 
     def halo_exchange(src, dst, sems, top, lead, starting):
@@ -381,11 +384,16 @@
         return g_s[...] + ly_s[...] * above[None] + ry_s[...] * below[None], above, below
 
     v, above, below = y_half(0)
-    r = x_source(v, above, below)
-    for n, s in enumerate(strides_of(X)):
-        r = wx_s[n, 0] * r + wx_s[n, 1] * pltpu.roll(r, s, 2) + wx_s[n, 2] * pltpu.roll(r, X - s, 2)
-    g_s[...] = r
-    x_exchange(1, pack_edges(jnp.zeros((Z, X), jnp.float32), 0, r, 0))
+    g_s[...] = x_source(v, above, below)
+    packed = jnp.zeros((Z, X), jnp.float32)
+    for lo in range(0, Y, CH2):
+        part = slice(lo, lo + CH2)
+        r = g_s[part]
+        for n, s in enumerate(strides_of(X)):
+            r = wx_s[n, 0, part] * r + wx_s[n, 1, part] * pltpu.roll(r, s, 2) + wx_s[n, 2, part] * pltpu.roll(r, X - s, 2)
+        g_s[part] = r
+        packed = pack_edges(packed, lo, r, 0)
+    x_exchange(1, packed)
     v, above, below = y_half(1)
 
     change = v - q_s[...]
@@ -399,6 +407,8 @@
     halo_exchange(rown, rbuf, sr, 2, 0, True)
     for j in range(Y):
         op_ref[pl.ds(j, Z, stride=Y), :] = v[j]
+    out_p = pltpu.make_async_copy(op_ref, op_hbm, sout.at[0])
+    out_p.start()
 
     halo_exchange(cown, cbuf, sc, 3, 1, False)
 
@@ -465,6 +475,8 @@
     for j in range(CY):
         flip[pl.ds(j, CZ, stride=CY), :] = own[j]
     or_ref[...] = flip[0:CZ * CY, :half]
+    out_r = pltpu.make_async_copy(or_ref, or_hbm, sout.at[1])
+    out_r.start()
     for i in x_peers:
         await_recv(fown, fbuf.at[i], ssem, sf.at[i], (i, gy))
     for t in range(nx // 2):
@@ -475,15 +487,24 @@
         for j in range(CY):
             flip[pl.ds(base + j, CZ, stride=CY), :] = top[j] if j < hj else low[j - hj]
         oc_ref[:, t * X:(t + 1) * X] = flip[base:base + CZ * CY, :]
+    out_c = pltpu.make_async_copy(oc_ref, oc_hbm, sout.at[2])
+    out_c.start()
     comm.finish()
+    out_p.wait()
+    out_r.wait()
+    out_c.wait()
 
 
 def put(*refs):
-    sems = refs[6]
-    copies = [pltpu.make_async_copy(refs[m], refs[3 + m], sems.at[m]) for m in range(3)]
-    for copy in copies:
+    sems = refs[9]
+    take = [pltpu.make_async_copy(refs[m], refs[6 + m], sems.at[m]) for m in range(3)]
+    give = [pltpu.make_async_copy(refs[6 + m], refs[3 + m], sems.at[3 + m]) for m in range(3)]
+    for copy in take:
         copy.start()
-    for copy in copies:
+    for m in range(3):
+        take[m].wait()
+        give[m].start()
+    for copy in give:
         copy.wait()
 
 
@@ -503,7 +524,7 @@
     sends = 3 + (ny - 1) * 3 + (nx - 1) * 3 + 8 * 2
     dma = pltpu.SemaphoreType.DMA
     scratch = (
-        [vm(*block) for _ in range(11)]
+        [vm(*block) for _ in range(12)]
         + [vm(*block), vm(*block), vm(nsx, 3, *block), vm(*block), vm(*block), vm(nsy, 3, *block)]
         + [vm(Z, X), vm(3, Z, X), vm(Z, X), vm(2, Z, X), vm(1, Z, X)]
         + [vm(2, nx, Z, X), vm(2, Z, X), vm(ny, 4, Z, X), vm(4, Z, X), vm(2, ny, Z, X), vm(2, 2, Z, X)]
@@ -512,6 +533,7 @@
            vm(CY // 2, CZ, X), vm(nx, CY // 2, CZ, X), vm((nx // 2 + 1) * CZ * CY, X)]
         + [dma((sends,)), dma((3,)), dma((2, nx)), dma((ny,)), dma((2, ny)), dma((3, 3)), dma((3, 3)), dma((nx,))]
         + [vm(6, Z * Y, X), dma((6,))]
+        + [vm(Z * Y, X), vm(CZ * CY, X // 2), vm(CZ * CY, nx * X // 2), dma((3,))]
     )
     p, r, c = pl.pallas_call(
         functools.partial(kernel, nx, ny),
@@ -521,12 +543,20 @@
             jax.ShapeDtypeStruct((CZ * CY, nx * X // 2), f32),
         ),
         in_specs=[pl.BlockSpec(memory_space=pltpu.HBM)] * 6,
-        out_specs=[pl.BlockSpec(memory_space=pltpu.VMEM)] * 3,
+        out_specs=[pl.BlockSpec(memory_space=pltpu.HBM)] * 3,
         scratch_shapes=scratch,
         compiler_params=pltpu.CompilerParams(
             collective_id=0, has_side_effects=True, vmem_limit_bytes=67043328
         ),
     )(*flat)
+    p, r, c = pl.pallas_call(
+        put,
+        out_shape=tuple(jax.ShapeDtypeStruct(v.shape, f32) for v in (p, r, c)),
+        in_specs=[pl.BlockSpec(memory_space=pltpu.HBM)] * 3,
+        out_specs=[pl.BlockSpec(memory_space=pltpu.HBM)] * 3,
+        scratch_shapes=[pltpu.VMEM(v.shape, f32) for v in (p, r, c)] + [dma((6,))],
+        compiler_params=pltpu.CompilerParams(vmem_limit_bytes=67043328),
+    )(p, r, c)
     return p.reshape(Z, Y, X), r.reshape(CZ, CY, X // 2), c.reshape(CZ, CY, nx * X // 2)
 
 

time: 39.1 us -> 37.4 us (0.957)
  local copies, waits for them, and re-layouts: 3.06 us -> 0 us
  Pallas kernels: 34.8 us -> 36.2 us
    unnamed x7 -> x0, local copies, waits for them, and re-layouts: 3.06 us -> none
    pallas_call x0 -> x1, Pallas kernels: none -> 1.64 us  [body(): pl.pallas_call(put, out_shape=tuple((jax.ShapeDtypeStruct(v.shape, f32) f...]
where the time goes in v3:
time: 37.4 us; the launch traced here: 36.9 us
  Pallas kernels  36.2 us (97%)
  between operations  0.64 us (2%)
    pallas_call x1, Pallas kernels, body(): pl.pallas_call(functools.partial(kernel, nx, ny), out_shape=(jax.ShapeDty...  34.6 us
    pallas_call x1, Pallas kernels, body(): pl.pallas_call(put, out_shape=tuple((jax.ShapeDtypeStruct(v.shape, f32) f...  1.64 us

profile of v3, /device:TPU:1, one launch (start us, length us, event | category | flops | bytes accessed | tf_op | source)
XLA Modules:
  0.0 36.9 jit_solution(10682344407333922380)
XLA Ops:
  0.6 34.6 %shard_map.85 = (f32[256,128]{1,0:T(8,128)}, f32[64,64]{1,0:T(8,128)}, f32[64,256]{1,0:T(8,128)}) custom-call(f32[256,128]{1,0:T(8,128)} %bitcast.9, f32[256,128]{1,0:T(8,128)} %bitcast.10, f32[256,128]{1,0:T(8,128)} %bitcast.11, f32[256,128]{1,0:T(8,128)} %bitcast.12, f32[256,128]{1,0:T(8,128)} %bitcast.13, f32[256,128]{1,0:T(8,128)} %bitcast.14), custom_call_target="tpu_custom_call" | custom-call | tf_op jit(solution)/shard_map/pallas_call | solution.py:538
  35.2 1.6 %shard_map.86 = (f32[256,128]{1,0:T(8,128)}, f32[64,64]{1,0:T(8,128)}, f32[64,256]{1,0:T(8,128)}) custom-call(f32[256,128]{1,0:T(8,128)} %get-tuple-element.9.refs_0_, f32[64,64]{1,0:T(8,128)} %get-tuple-element.10.refs_1_, f32[64,256]{1,0:T(8,128)} %get-tuple-element.11.refs_2_), custom_call_target="tpu_custom_call" | custom-call | tf_op jit(solution)/shard_map/pallas_call | solution.py:552
